TPU v7x, 32 devices: a whole 2x2x4 slice. The times are simulated.
32 devices in a mesh: stream: 4 (over z), trans: 8 (over y, x, core).
Axes of the slice: x: 2, y: 2, z: 4, core: 2. Of those that a mesh axis runs over, the one named last changes fastest.
Arguments:
- rhs: float32 [64, 128, 128], P('stream', 'trans'), may hold values from -60 to 60
- vof: int32 [64, 128, 128], P('stream', 'trans'), may hold values from 0 to 1000
- disc_owner: int32 [4, 2048, 1], P('stream', 'trans'), may hold values from 0 to 7; in each aligned block of 256 rows (0 to 255, 256 to 511, ..., all dimensions but the last counted through in order) at most 32 rows name the same one
- disc_cell: int32 [4, 2048], P('stream', 'trans'), may hold values from 0 to 32767
- disc_force: float32 [4, 2048], P('stream', 'trans'), may hold values from -240 to 240
Outputs:
- pressure: float32 [64, 128, 128], P('stream', 'trans')
Inputs may be any that keep to these rules, and one draw needn't show every extreme that they name: `disc_owner`: among the 256 rows of one device at most 32 name the same owner, and on some device exactly 32 rows name one owner.
All inputs are finite; a program needn't handle non-finite values.
Results may differ from a plain program's by a relative error of at most 0.0001.
Values sent between devices are 32-bit elements; how exact they have to be, the bound alone decides.
No kernel may reach another device: no remote copies, remote signals or barrier semaphores. Data moves between devices by JAX's collectives and lax.ppermute only.
A program may use at most 192 MiB of HBM per device.

v0:
```python
import jax
import jax.numpy as jnp
from jax import lax
from jax.sharding import PartitionSpec as P

LEVELS = 4
POST = 2
CSWEEPS = 8
CAP = 32


air_density = 0.0012
omega_factor = 0.8


def with_halo(cells, sides, width):
    for axis, dim in sides:
        count = lax.axis_size(axis)
        ends = count - 1
        head = lax.slice_in_dim(cells, 0, width, axis=dim)
        tail = lax.slice_in_dim(cells, cells.shape[dim] - width, cells.shape[dim], axis=dim)
        cells = jnp.concatenate(
            [
                lax.ppermute(tail, axis, [(i, (i + 1) % count) for i in range(ends)]),
                cells,
                lax.ppermute(head, axis, [((i + 1) % count, i) for i in range(ends)]),
            ],
            axis=dim,
        )
    return cells


def neighbour_slices(padded):
    return (
        padded[2:, 1:-1, 1:-1],
        padded[:-2, 1:-1, 1:-1],
        padded[1:-1, 2:, 1:-1],
        padded[1:-1, :-2, 1:-1],
        padded[1:-1, 1:-1, 2:],
        padded[1:-1, 1:-1, :-2],
    )


def face_terms(density, padded, scale):
    faces = tuple((scale * 2.0 / (density + other) for other in neighbour_slices(padded)))
    total = faces[0] + faces[1] + faces[2] + faces[3] + faces[4] + faces[5]
    return (faces, total)


def apply_op(padded, field, faces, total):
    near = neighbour_slices(padded)
    beside = faces[0] * near[0] + faces[1] * near[1] + faces[2] * near[2]
    beside = beside + faces[3] * near[3] + faces[4] * near[4] + faces[5] * near[5]
    return total * field - beside


def pad_depth(extended):
    return jnp.pad(extended, ((0, 0), (0, 0), (1, 1)))


def density_halo(density):
    return pad_depth(with_halo(density, (("stream", 0), ("trans", 1)), 1))


def field_halo(field):
    return pad_depth(with_halo(field, (("stream", 0), ("trans", 1)), 1))


def coarse_halo(field):
    return pad_depth(with_halo(field, (("stream", 0), ("trans", 1)), 1))


def sweep(field, level_rhs, faces, total, halo_fn):
    return (
        field + omega_factor * (level_rhs - apply_op(halo_fn(field), field, faces, total)) / total
    )


def coarsen(field):
    depth_x, depth_y, depth_z = field.shape
    return field.reshape(depth_x // 2, 2, depth_y // 2, 2, depth_z // 2, 2).mean(axis=(1, 3, 5))


def refine(field):
    depth_x, depth_y, depth_z = field.shape
    wide = jnp.broadcast_to(field[:, None, :, None, :, None], (depth_x, 2, depth_y, 2, depth_z, 2))
    return wide.reshape(2 * depth_x, 2 * depth_y, 2 * depth_z)


def body(rhs, vof, disc_owner, disc_cell, disc_force):
    cell_count = rhs.shape[0] * rhs.shape[1] * rhs.shape[2]
    groups = lax.axis_size("trans")
    owner = disc_owner[0, :, 0]
    cell_ids = disc_cell[0]
    forces = disc_force[0]
    member = (owner[:, None] == jnp.arange(groups, dtype=jnp.int32)[None, :]).astype(jnp.int32)
    ranks = jnp.sum((jnp.cumsum(member, axis=0) - 1) * member, axis=1)
    target = owner * CAP + ranks
    payload = jnp.stack([cell_ids.astype(jnp.float32), forces])
    packed = jnp.zeros((2, groups * CAP), jnp.float32).at[:, target].set(payload)
    arrived = lax.all_to_all(
        packed.reshape(2, groups, CAP), "trans", split_axis=1, concat_axis=1, tiled=True
    )
    arrived = arrived.reshape(2, groups * CAP)
    local_cell = arrived[0].astype(jnp.int32)
    local_force = arrived[1]
    source = (
        jnp.zeros((cell_count,), jnp.float32).at[local_cell].add(local_force).reshape(rhs.shape)
    )
    level_rhs = rhs + source
    density = air_density + (1.0 - air_density) * (vof.astype(jnp.float32) / 1000.0)
    merge_at = LEVELS
    operators = []
    for level in range(merge_at):
        if level > 0:
            density = coarsen(density)
        operators.append((density, density_halo(density), 0.25**level))
    density = coarsen(density)
    stored = []
    for level in range(merge_at):
        faces, total = face_terms(*operators[level])
        field = omega_factor * level_rhs / total
        field = sweep(field, level_rhs, faces, total, field_halo)
        residual = level_rhs - apply_op(field_halo(field), field, faces, total)
        stored.append((field, level_rhs))
        level_rhs = coarsen(residual)
    faces, total = face_terms(density, density_halo(density), 0.25**LEVELS)
    field = omega_factor * level_rhs / total
    for repeat in range(CSWEEPS - 1):
        field = sweep(field, level_rhs, faces, total, coarse_halo)
    for level in range(merge_at - 1, -1, -1):
        faces, total = face_terms(*operators[level])
        upper, upper_rhs = stored[level]
        field = upper + refine(field)
        for repeat in range(POST):
            field = sweep(field, upper_rhs, faces, total, field_halo)
    return field


def solution(mesh):
    return jax.shard_map(
        body,
        mesh=mesh,
        in_specs=(
            P("stream", "trans", None),
            P("stream", "trans", None),
            P("stream", "trans", None),
            P("stream", "trans"),
            P("stream", "trans"),
        ),
        out_specs=P("stream", "trans", None),
        check_vma=False,
    )
```

profile of v0, /device:TPU:0, one launch (start us, length us, event | category | flops | bytes accessed | tf_op | source)
XLA Modules:
  0.0 464.3 jit_solution(9658475761666708825)
XLA Ops:
  6.4 5.2 %all-to-all-start = ((f32[2,8,32]{2,0,1:T(2,128)}), f32[2,8,32]{2,0,1:T(2,128)S(1)}, u32[]{:S(2)}, u32[]{:S(2)}) async-start(f32[2,8,32]{2,0,1:T(2,128)} %copy.10), calls=%async_computation | async-start | bytes 16384 | tf_op jit(solution)/shard_map/all_to_all | solution.py:101
  12.5 3.5 collective-permute-start.1
  17.5 9.8 %reshape.156 = f32[8,2,8,2,64,2]{5,4,3,2,1,0:T(8,128)} reshape(f32[16,16,128]{2,1,0:T(8,128)S(1)} %multiply_add_fusion) | data formatting | bytes 262144 | tf_op jit(solution)/shard_map/reshape | solution.py:81
  27.2 4.0 reduce_sum.100
  38.5 4.5 collective-permute-start.5
  44.4 4.5 collective-permute-start.13
  51.5 3.5 collective-permute-start.7
  59.8 4.5 collective-permute-start.9
  65.7 4.0 collective-permute-start.15
  75.5 4.0 collective-permute-done.10
  80.0 9.8 %reshape.155 = f32[8,2,8,2,64,2]{5,4,3,2,1,0:T(8,128)} reshape(f32[16,16,128]{2,1,0:T(8,128)S(1)} %fusion.31) | data formatting | bytes 262144 | tf_op jit(solution)/shard_map/reshape | solution.py:81
  89.8 4.0 reduce_sum.99
  93.9 4.3 collective-permute-start.17
  99.5 4.5 collective-permute-start.25
  105.6 3.5 collective-permute-start.19
  113.5 4.5 collective-permute-start.21
  119.4 4.5 collective-permute-start.27
  125.2 3.3 collective-permute-start.23
  130.0 4.1 collective-permute-done.22
  135.7 4.3 collective-permute-start.29
  141.3 4.7 %collective-permute-start.37 = (f32[1,2,16]{2,1,0:T(2,128)S(1)}, f32[1,2,16]{2,1,0:T(2,128)S(1)}, u32[]{:S(2)}, u32[]{:S(2)}) collective-permute-start(f32[1,2,16]{2,1,0:T(2,128)S(1)} %get-tuple-element.106), channel_id=1, source_target_pairs={{0,8},{8,16},{16,24},{1,9},{9,17},{17,25},{2,10},{10,18},{18,26},{... | collective-permute-start | bytes 392 | tf_op jit(solution)/shard_map/ppermute | solution.py:24
  147.4 3.4 collective-permute-start.31
  155.2 4.5 collective-permute-start.33
  161.1 4.4 collective-permute-start.39
  166.9 3.4 collective-permute-start.35
  171.6 4.1 collective-permute-done.34
  176.5 4.3 collective-permute-start.49
  180.7 3.5 collective-permute-start.41
  193.6 5.1 %collective-permute-start.51 = (f32[3,1,8]{2,1,0:T(1,128)S(1)}, f32[3,1,8]{2,1,0:T(1,128)S(1)}, u32[]{:S(2)}, u32[]{:S(2)}) collective-permute-start(f32[3,1,8]{2,1,0:T(1,128)S(1)} %pad_maximum_fusion.210), channel_id=1, source_target_pairs={{0,1},{1,2},{2,3},{3,4},{4,5},{5,6},{6,7},{8,9},{9,10},{10,11},{11... | collective-permute-start | bytes 296 | tf_op jit(solution)/shard_map/ppermute | solution.py:24
  199.0 3.4 collective-permute-start.45
  211.5 4.1 collective-permute-done.46
  220.3 4.2 collective-permute-done.52
  228.6 4.6 collective-permute-done.54
  237.5 4.2 collective-permute-done.56
  245.8 3.5 collective-permute-done.58
  249.5 3.4 collective-permute-start.61
  254.3 4.2 collective-permute-done.60
  262.6 3.5 collective-permute-done.62
  269.6 4.2 collective-permute-done.64
  278.2 3.3 collective-permute-done.66
  284.9 4.2 collective-permute-done.68
  293.5 3.3 collective-permute-done.70
  300.2 4.2 collective-permute-done.72
  308.8 3.3 collective-permute-done.74
  315.5 4.2 collective-permute-done.76
  324.1 3.3 collective-permute-done.78
  331.0 4.2 collective-permute-done.80
  339.6 3.3 collective-permute-done.82
  346.3 4.2 collective-permute-done.84
  355.0 3.3 collective-permute-done.86
  361.9 4.2 collective-permute-done.88
  370.6 3.3 collective-permute-done.90
  377.3 4.2 collective-permute-done.92
  385.9 3.3 collective-permute-done.94
  393.5 4.2 collective-permute-done.96
  402.2 3.3 collective-permute-done.98
  408.9 4.2 collective-permute-done.100
  417.7 3.2 collective-permute-done.102
  421.1 3.9 broadcast_in_dim.47
  425.1 6.9 %reshape.161 = f32[16,16,128]{2,1,0:T(8,128)S(1)} reshape(f32[8,2,8,2,64,2]{5,4,3,2,1,0:T(8,128)} %broadcast_in_dim.47) | data formatting | bytes 262144 | tf_op jit(solution)/shard_map/reshape | solution.py:87
  435.3 4.2 collective-permute-done.104
  444.0 3.2 collective-permute-done.106
  451.1 4.2 collective-permute-done.108
  455.3 3.3 collective-permute-start.111
  (326 shorter events, 195.2 us)
Async XLA Ops:
  6.4 24.9 %all-to-all-start = ((f32[2,8,32]{2,0,1:T(2,128)}), f32[2,8,32]{2,0,1:T(2,128)S(1)}, u32[]{:S(2)}, u32[]{:S(2)}) async-start(f32[2,8,32]{2,0,1:T(2,128)} %copy.10), calls=%async_computation | async-start | bytes 16384 | tf_op jit(solution)/shard_map/all_to_all | solution.py:101
  12.5 18.9 %collective-permute-start.1 = (f32[1,16,128]{2,1,0:T(8,128)S(1)}, f32[1,16,128]{2,1,0:T(8,128)S(1)}, u32[]{:S(2)}, u32[]{:S(2)}) collective-permute-start(f32[1,16,128]{2,1,0:T(8,128)S(1)} %get-tuple-element.45), channel_id=1, source_target_pairs={{0,8},{8,16},{16,24},{1,9},{9,17},{17,25},{2,10},{10,18},{18,26},{... | collective-permute-start | bytes 24584 | tf_op jit(solution)/shard_map/ppermute | solution.py:24
  16.0 15.3 %collective-permute-start = (f32[1,16,128]{2,1,0:T(8,128)S(1)}, f32[1,16,128]{2,1,0:T(8,128)S(1)}, u32[]{:S(2)}, u32[]{:S(2)}) collective-permute-start(f32[1,16,128]{2,1,0:T(8,128)S(1)} %get-tuple-element.46), channel_id=1, source_target_pairs={{8,0},{16,8},{24,16},{9,1},{17,9},{25,17},{10,2},{18,10},{26,18},{... | collective-permute-start | bytes 24584 | tf_op jit(solution)/shard_map/ppermute | solution.py:26
  31.4 5.5 %collective-permute-start.3 = (f32[18,1,128]{2,1,0:T(1,128)S(1)}, f32[18,1,128]{2,1,0:T(1,128)S(1)}, u32[]{:S(2)}, u32[]{:S(2)}) collective-permute-start(f32[18,1,128]{2,1,0:T(1,128)S(1)} %get-tuple-element.35), channel_id=1, source_target_pairs={{0,1},{1,2},{2,3},{3,4},{4,5},{5,6},{6,7},{8,9},{9,10},{10,11},{11... | collective-permute-start | bytes 27656 | tf_op jit(solution)/shard_map/ppermute | solution.py:24
  38.5 13.0 %collective-permute-start.5 = (f32[1,16,128]{2,1,0:T(8,128)S(1)}, f32[1,16,128]{2,1,0:T(8,128)S(1)}, u32[]{:S(2)}, u32[]{:S(2)}) collective-permute-start(f32[1,16,128]{2,1,0:T(8,128)S(1)} %get-tuple-element.43), channel_id=1, source_target_pairs={{0,8},{8,16},{16,24},{1,9},{9,17},{17,25},{2,10},{10,18},{18,26},{... | collective-permute-start | bytes 24584 | tf_op jit(solution)/shard_map/ppermute | solution.py:24
  43.1 8.4 %collective-permute-start.4 = (f32[1,16,128]{2,1,0:T(8,128)S(1)}, f32[1,16,128]{2,1,0:T(8,128)S(1)}, u32[]{:S(2)}, u32[]{:S(2)}) collective-permute-start(f32[1,16,128]{2,1,0:T(8,128)S(1)} %get-tuple-element.44), channel_id=1, source_target_pairs={{8,0},{16,8},{24,16},{9,1},{17,9},{25,17},{10,2},{18,10},{26,18},{... | collective-permute-start | bytes 24584 | tf_op jit(solution)/shard_map/ppermute | solution.py:26
  44.4 21.2 %collective-permute-start.13 = (f32[1,8,64]{2,1,0:T(8,128)S(1)}, f32[1,8,64]{2,1,0:T(8,128)S(1)}, u32[]{:S(2)}, u32[]{:S(2)}) collective-permute-start(f32[1,8,64]{2,1,0:T(8,128)S(1)} %get-tuple-element.65), channel_id=1, source_target_pairs={{0,8},{8,16},{16,24},{1,9},{9,17},{17,25},{2,10},{10,18},{18,26},{... | collective-permute-start | bytes 6152 | tf_op jit(solution)/shard_map/ppermute | solution.py:24
  49.0 16.7 %collective-permute-start.12 = (f32[1,8,64]{2,1,0:T(8,128)S(1)}, f32[1,8,64]{2,1,0:T(8,128)S(1)}, u32[]{:S(2)}, u32[]{:S(2)}) collective-permute-start(f32[1,8,64]{2,1,0:T(8,128)S(1)} %get-tuple-element.66), channel_id=1, source_target_pairs={{8,0},{16,8},{24,16},{9,1},{17,9},{25,17},{10,2},{18,10},{26,18},{... | collective-permute-start | bytes 6152 | tf_op jit(solution)/shard_map/ppermute | solution.py:26
  51.5 4.8 %collective-permute-start.7 = (f32[18,1,128]{2,1,0:T(1,128)S(1)}, f32[18,1,128]{2,1,0:T(1,128)S(1)}, u32[]{:S(2)}, u32[]{:S(2)}) collective-permute-start(f32[18,1,128]{2,1,0:T(1,128)S(1)} %get-tuple-element.33), channel_id=1, source_target_pairs={{0,1},{1,2},{2,3},{3,4},{4,5},{5,6},{6,7},{8,9},{9,10},{10,11},{11... | collective-permute-start | bytes 27656 | tf_op jit(solution)/shard_map/ppermute | solution.py:24
  59.8 11.2 %collective-permute-start.9 = (f32[1,16,128]{2,1,0:T(8,128)S(1)}, f32[1,16,128]{2,1,0:T(8,128)S(1)}, u32[]{:S(2)}, u32[]{:S(2)}) collective-permute-start(f32[1,16,128]{2,1,0:T(8,128)S(1)} %get-tuple-element.41), channel_id=1, source_target_pairs={{0,8},{8,16},{16,24},{1,9},{9,17},{17,25},{2,10},{10,18},{18,26},{... | collective-permute-start | bytes 24584 | tf_op jit(solution)/shard_map/ppermute | solution.py:24
  64.3 6.7 %collective-permute-start.8 = (f32[1,16,128]{2,1,0:T(8,128)S(1)}, f32[1,16,128]{2,1,0:T(8,128)S(1)}, u32[]{:S(2)}, u32[]{:S(2)}) collective-permute-start(f32[1,16,128]{2,1,0:T(8,128)S(1)} %get-tuple-element.42), channel_id=1, source_target_pairs={{8,0},{16,8},{24,16},{9,1},{17,9},{25,17},{10,2},{18,10},{26,18},{... | collective-permute-start | bytes 24584 | tf_op jit(solution)/shard_map/ppermute | solution.py:26
  65.7 9.7 %collective-permute-start.15 = (f32[10,1,64]{2,1,0:T(1,128)S(1)}, f32[10,1,64]{2,1,0:T(1,128)S(1)}, u32[]{:S(2)}, u32[]{:S(2)}) collective-permute-start(f32[10,1,64]{2,1,0:T(1,128)S(1)} %get-tuple-element.55), channel_id=1, source_target_pairs={{0,1},{1,2},{2,3},{3,4},{4,5},{5,6},{6,7},{8,9},{9,10},{10,11},{11... | collective-permute-start | bytes 7688 | tf_op jit(solution)/shard_map/ppermute | solution.py:24
  69.7 5.7 %collective-permute-start.14 = (f32[10,1,64]{2,1,0:T(1,128)S(1)}, f32[10,1,64]{2,1,0:T(1,128)S(1)}, u32[]{:S(2)}, u32[]{:S(2)}) collective-permute-start(f32[10,1,64]{2,1,0:T(1,128)S(1)} %get-tuple-element.56), channel_id=1, source_target_pairs={{1,0},{2,1},{3,2},{4,3},{5,4},{6,5},{7,6},{9,8},{10,9},{11,10},{12... | collective-permute-start | bytes 7688 | tf_op jit(solution)/shard_map/ppermute | solution.py:26
  74.1 5.5 %collective-permute-start.10 = (f32[18,1,128]{2,1,0:T(1,128)S(1)}, f32[18,1,128]{2,1,0:T(1,128)S(1)}, u32[]{:S(2)}, u32[]{:S(2)}) collective-permute-start(f32[18,1,128]{2,1,0:T(1,128)S(1)} %get-tuple-element.32), channel_id=1, source_target_pairs={{1,0},{2,1},{3,2},{4,3},{5,4},{6,5},{7,6},{9,8},{10,9},{11,10},{12... | collective-permute-start | bytes 27656 | tf_op jit(solution)/shard_map/ppermute | solution.py:26
  93.9 11.7 %collective-permute-start.17 = (f32[1,8,64]{2,1,0:T(8,128)S(1)}, f32[1,8,64]{2,1,0:T(8,128)S(1)}, u32[]{:S(2)}, u32[]{:S(2)}) collective-permute-start(f32[1,8,64]{2,1,0:T(8,128)S(1)} %get-tuple-element.63), channel_id=1, source_target_pairs={{0,8},{8,16},{16,24},{1,9},{9,17},{17,25},{2,10},{10,18},{18,26},{... | collective-permute-start | bytes 6152 | tf_op jit(solution)/shard_map/ppermute | solution.py:24
  98.2 7.4 %collective-permute-start.16 = (f32[1,8,64]{2,1,0:T(8,128)S(1)}, f32[1,8,64]{2,1,0:T(8,128)S(1)}, u32[]{:S(2)}, u32[]{:S(2)}) collective-permute-start(f32[1,8,64]{2,1,0:T(8,128)S(1)} %get-tuple-element.64), channel_id=1, source_target_pairs={{8,0},{16,8},{24,16},{9,1},{17,9},{25,17},{10,2},{18,10},{26,18},{... | collective-permute-start | bytes 6152 | tf_op jit(solution)/shard_map/ppermute | solution.py:26
  99.5 19.9 %collective-permute-start.25 = (f32[1,4,32]{2,1,0:T(4,128)S(1)}, f32[1,4,32]{2,1,0:T(4,128)S(1)}, u32[]{:S(2)}, u32[]{:S(2)}) collective-permute-start(f32[1,4,32]{2,1,0:T(4,128)S(1)} %get-tuple-element.85), channel_id=1, source_target_pairs={{0,8},{8,16},{16,24},{1,9},{9,17},{17,25},{2,10},{10,18},{18,26},{... | collective-permute-start | bytes 1544 | tf_op jit(solution)/shard_map/ppermute | solution.py:24
  104.1 15.3 %collective-permute-start.24 = (f32[1,4,32]{2,1,0:T(4,128)S(1)}, f32[1,4,32]{2,1,0:T(4,128)S(1)}, u32[]{:S(2)}, u32[]{:S(2)}) collective-permute-start(f32[1,4,32]{2,1,0:T(4,128)S(1)} %get-tuple-element.86), channel_id=1, source_target_pairs={{8,0},{16,8},{24,16},{9,1},{17,9},{25,17},{10,2},{18,10},{26,18},{... | collective-permute-start | bytes 1544 | tf_op jit(solution)/shard_map/ppermute | solution.py:26
  105.6 4.8 %collective-permute-start.19 = (f32[10,1,64]{2,1,0:T(1,128)S(1)}, f32[10,1,64]{2,1,0:T(1,128)S(1)}, u32[]{:S(2)}, u32[]{:S(2)}) collective-permute-start(f32[10,1,64]{2,1,0:T(1,128)S(1)} %get-tuple-element.53), channel_id=1, source_target_pairs={{0,1},{1,2},{2,3},{3,4},{4,5},{5,6},{6,7},{8,9},{9,10},{10,11},{11... | collective-permute-start | bytes 7688 | tf_op jit(solution)/shard_map/ppermute | solution.py:24
  113.5 11.7 %collective-permute-start.21 = (f32[1,8,64]{2,1,0:T(8,128)S(1)}, f32[1,8,64]{2,1,0:T(8,128)S(1)}, u32[]{:S(2)}, u32[]{:S(2)}) collective-permute-start(f32[1,8,64]{2,1,0:T(8,128)S(1)} %get-tuple-element.61), channel_id=1, source_target_pairs={{0,8},{8,16},{16,24},{1,9},{9,17},{17,25},{2,10},{10,18},{18,26},{... | collective-permute-start | bytes 6152 | tf_op jit(solution)/shard_map/ppermute | solution.py:24
  118.1 7.1 %collective-permute-start.20 = (f32[1,8,64]{2,1,0:T(8,128)S(1)}, f32[1,8,64]{2,1,0:T(8,128)S(1)}, u32[]{:S(2)}, u32[]{:S(2)}) collective-permute-start(f32[1,8,64]{2,1,0:T(8,128)S(1)} %get-tuple-element.62), channel_id=1, source_target_pairs={{8,0},{16,8},{24,16},{9,1},{17,9},{25,17},{10,2},{18,10},{26,18},{... | collective-permute-start | bytes 6152 | tf_op jit(solution)/shard_map/ppermute | solution.py:26
  119.4 10.4 %collective-permute-start.27 = (f32[6,1,32]{2,1,0:T(1,128)S(1)}, f32[6,1,32]{2,1,0:T(1,128)S(1)}, u32[]{:S(2)}, u32[]{:S(2)}) collective-permute-start(f32[6,1,32]{2,1,0:T(1,128)S(1)} %get-tuple-element.75), channel_id=1, source_target_pairs={{0,1},{1,2},{2,3},{3,4},{4,5},{5,6},{6,7},{8,9},{9,10},{10,11},{11... | collective-permute-start | bytes 2312 | tf_op jit(solution)/shard_map/ppermute | solution.py:24
  123.9 6.0 %collective-permute-start.26 = (f32[6,1,32]{2,1,0:T(1,128)S(1)}, f32[6,1,32]{2,1,0:T(1,128)S(1)}, u32[]{:S(2)}, u32[]{:S(2)}) collective-permute-start(f32[6,1,32]{2,1,0:T(1,128)S(1)} %get-tuple-element.76), channel_id=1, source_target_pairs={{1,0},{2,1},{3,2},{4,3},{5,4},{6,5},{7,6},{9,8},{10,9},{11,10},{12... | collective-permute-start | bytes 2312 | tf_op jit(solution)/shard_map/ppermute | solution.py:26
  128.6 5.6 %collective-permute-start.22 = (f32[10,1,64]{2,1,0:T(1,128)S(1)}, f32[10,1,64]{2,1,0:T(1,128)S(1)}, u32[]{:S(2)}, u32[]{:S(2)}) collective-permute-start(f32[10,1,64]{2,1,0:T(1,128)S(1)} %get-tuple-element.52), channel_id=1, source_target_pairs={{1,0},{2,1},{3,2},{4,3},{5,4},{6,5},{7,6},{9,8},{10,9},{11,10},{12... | collective-permute-start | bytes 7688 | tf_op jit(solution)/shard_map/ppermute | solution.py:26
  135.7 11.6 %collective-permute-start.29 = (f32[1,4,32]{2,1,0:T(4,128)S(1)}, f32[1,4,32]{2,1,0:T(4,128)S(1)}, u32[]{:S(2)}, u32[]{:S(2)}) collective-permute-start(f32[1,4,32]{2,1,0:T(4,128)S(1)} %get-tuple-element.83), channel_id=1, source_target_pairs={{0,8},{8,16},{16,24},{1,9},{9,17},{17,25},{2,10},{10,18},{18,26},{... | collective-permute-start | bytes 1544 | tf_op jit(solution)/shard_map/ppermute | solution.py:24
  140.0 7.4 %collective-permute-start.28 = (f32[1,4,32]{2,1,0:T(4,128)S(1)}, f32[1,4,32]{2,1,0:T(4,128)S(1)}, u32[]{:S(2)}, u32[]{:S(2)}) collective-permute-start(f32[1,4,32]{2,1,0:T(4,128)S(1)} %get-tuple-element.84), channel_id=1, source_target_pairs={{8,0},{16,8},{24,16},{9,1},{17,9},{25,17},{10,2},{18,10},{26,18},{... | collective-permute-start | bytes 1544 | tf_op jit(solution)/shard_map/ppermute | solution.py:26
  141.3 10.8 %collective-permute-start.37 = (f32[1,2,16]{2,1,0:T(2,128)S(1)}, f32[1,2,16]{2,1,0:T(2,128)S(1)}, u32[]{:S(2)}, u32[]{:S(2)}) collective-permute-start(f32[1,2,16]{2,1,0:T(2,128)S(1)} %get-tuple-element.106), channel_id=1, source_target_pairs={{0,8},{8,16},{16,24},{1,9},{9,17},{17,25},{2,10},{10,18},{18,26},{... | collective-permute-start | bytes 392 | tf_op jit(solution)/shard_map/ppermute | solution.py:24
  146.0 6.1 %collective-permute-start.36 = (f32[1,2,16]{2,1,0:T(2,128)S(1)}, f32[1,2,16]{2,1,0:T(2,128)S(1)}, u32[]{:S(2)}, u32[]{:S(2)}) collective-permute-start(f32[1,2,16]{2,1,0:T(2,128)S(1)} %get-tuple-element.107), channel_id=1, source_target_pairs={{8,0},{16,8},{24,16},{9,1},{17,9},{25,17},{10,2},{18,10},{26,18},{... | collective-permute-start | bytes 392 | tf_op jit(solution)/shard_map/ppermute | solution.py:26
  147.4 4.8 %collective-permute-start.31 = (f32[6,1,32]{2,1,0:T(1,128)S(1)}, f32[6,1,32]{2,1,0:T(1,128)S(1)}, u32[]{:S(2)}, u32[]{:S(2)}) collective-permute-start(f32[6,1,32]{2,1,0:T(1,128)S(1)} %get-tuple-element.73), channel_id=1, source_target_pairs={{0,1},{1,2},{2,3},{3,4},{4,5},{5,6},{6,7},{8,9},{9,10},{10,11},{11... | collective-permute-start | bytes 2312 | tf_op jit(solution)/shard_map/ppermute | solution.py:24
  155.2 11.6 %collective-permute-start.33 = (f32[1,4,32]{2,1,0:T(4,128)S(1)}, f32[1,4,32]{2,1,0:T(4,128)S(1)}, u32[]{:S(2)}, u32[]{:S(2)}) collective-permute-start(f32[1,4,32]{2,1,0:T(4,128)S(1)} %get-tuple-element.81), channel_id=1, source_target_pairs={{0,8},{8,16},{16,24},{1,9},{9,17},{17,25},{2,10},{10,18},{18,26},{... | collective-permute-start | bytes 1544 | tf_op jit(solution)/shard_map/ppermute | solution.py:24
  159.8 7.0 %collective-permute-start.32 = (f32[1,4,32]{2,1,0:T(4,128)S(1)}, f32[1,4,32]{2,1,0:T(4,128)S(1)}, u32[]{:S(2)}, u32[]{:S(2)}) collective-permute-start(f32[1,4,32]{2,1,0:T(4,128)S(1)} %get-tuple-element.82), channel_id=1, source_target_pairs={{8,0},{16,8},{24,16},{9,1},{17,9},{25,17},{10,2},{18,10},{26,18},{... | collective-permute-start | bytes 1544 | tf_op jit(solution)/shard_map/ppermute | solution.py:26
  161.1 10.4 %collective-permute-start.39 = (f32[4,1,16]{2,1,0:T(1,128)S(1)}, f32[4,1,16]{2,1,0:T(1,128)S(1)}, u32[]{:S(2)}, u32[]{:S(2)}) collective-permute-start(f32[4,1,16]{2,1,0:T(1,128)S(1)} %get-tuple-element.95), channel_id=1, source_target_pairs={{0,1},{1,2},{2,3},{3,4},{4,5},{5,6},{6,7},{8,9},{9,10},{10,11},{11... | collective-permute-start | bytes 776 | tf_op jit(solution)/shard_map/ppermute | solution.py:24
  165.5 6.0 %collective-permute-start.38 = (f32[4,1,16]{2,1,0:T(1,128)S(1)}, f32[4,1,16]{2,1,0:T(1,128)S(1)}, u32[]{:S(2)}, u32[]{:S(2)}) collective-permute-start(f32[4,1,16]{2,1,0:T(1,128)S(1)} %get-tuple-element.96), channel_id=1, source_target_pairs={{1,0},{2,1},{3,2},{4,3},{5,4},{6,5},{7,6},{9,8},{10,9},{11,10},{12... | collective-permute-start | bytes 776 | tf_op jit(solution)/shard_map/ppermute | solution.py:26
  166.9 4.8 %collective-permute-start.35 = (f32[6,1,32]{2,1,0:T(1,128)S(1)}, f32[6,1,32]{2,1,0:T(1,128)S(1)}, u32[]{:S(2)}, u32[]{:S(2)}) collective-permute-start(f32[6,1,32]{2,1,0:T(1,128)S(1)} %get-tuple-element.71), channel_id=1, source_target_pairs={{0,1},{1,2},{2,3},{3,4},{4,5},{5,6},{6,7},{8,9},{9,10},{10,11},{11... | collective-permute-start | bytes 2312 | tf_op jit(solution)/shard_map/ppermute | solution.py:24
  170.2 5.5 %collective-permute-start.34 = (f32[6,1,32]{2,1,0:T(1,128)S(1)}, f32[6,1,32]{2,1,0:T(1,128)S(1)}, u32[]{:S(2)}, u32[]{:S(2)}) collective-permute-start(f32[6,1,32]{2,1,0:T(1,128)S(1)} %get-tuple-element.72), channel_id=1, source_target_pairs={{1,0},{2,1},{3,2},{4,3},{5,4},{6,5},{7,6},{9,8},{10,9},{11,10},{12... | collective-permute-start | bytes 2312 | tf_op jit(solution)/shard_map/ppermute | solution.py:26
  176.5 17.2 %collective-permute-start.49 = (f32[1,1,8]{2,1,0:T(1,128)S(1)}, f32[1,1,8]{2,1,0:T(1,128)S(1)}, u32[]{:S(2)}, u32[]{:S(2)}) collective-permute-start(f32[1,1,8]{2,1,0:T(1,128)S(1)} %multiply_bitcast_fusion), channel_id=1, source_target_pairs={{0,8},{8,16},{16,24},{1,9},{9,17},{17,25},{2,10},{10,18},{18,26},{... | collective-permute-start | bytes 104 | tf_op jit(solution)/shard_map/ppermute | solution.py:24
  180.7 6.1 %collective-permute-start.41 = (f32[1,2,16]{2,1,0:T(2,128)S(1)}, f32[1,2,16]{2,1,0:T(2,128)S(1)}, u32[]{:S(2)}, u32[]{:S(2)}) collective-permute-start(f32[1,2,16]{2,1,0:T(2,128)S(1)} %get-tuple-element.104), channel_id=1, source_target_pairs={{0,8},{8,16},{16,24},{1,9},{9,17},{17,25},{2,10},{10,18},{18,26},{... | collective-permute-start | bytes 392 | tf_op jit(solution)/shard_map/ppermute | solution.py:24
  184.3 5.5 %collective-permute-start.40 = (f32[1,2,16]{2,1,0:T(2,128)S(1)}, f32[1,2,16]{2,1,0:T(2,128)S(1)}, u32[]{:S(2)}, u32[]{:S(2)}) collective-permute-start(f32[1,2,16]{2,1,0:T(2,128)S(1)} %get-tuple-element.105), channel_id=1, source_target_pairs={{8,0},{16,8},{24,16},{9,1},{17,9},{25,17},{10,2},{18,10},{26,18},{... | collective-permute-start | bytes 392 | tf_op jit(solution)/shard_map/ppermute | solution.py:26
  185.6 8.1 %collective-permute-start.48 = (f32[1,1,8]{2,1,0:T(1,128)S(1)}, f32[1,1,8]{2,1,0:T(1,128)S(1)}, u32[]{:S(2)}, u32[]{:S(2)}) collective-permute-start(f32[1,1,8]{2,1,0:T(1,128)S(1)} %multiply_bitcast_fusion), channel_id=1, source_target_pairs={{8,0},{16,8},{24,16},{9,1},{17,9},{25,17},{10,2},{18,10},{26,18},{... | collective-permute-start | bytes 104 | tf_op jit(solution)/shard_map/ppermute | solution.py:26
  189.7 9.0 %collective-permute-start.43 = (f32[4,1,16]{2,1,0:T(1,128)S(1)}, f32[4,1,16]{2,1,0:T(1,128)S(1)}, u32[]{:S(2)}, u32[]{:S(2)}) collective-permute-start(f32[4,1,16]{2,1,0:T(1,128)S(1)} %get-tuple-element.93), channel_id=1, source_target_pairs={{0,1},{1,2},{2,3},{3,4},{4,5},{5,6},{6,7},{8,9},{9,10},{10,11},{11... | collective-permute-start | bytes 776 | tf_op jit(solution)/shard_map/ppermute | solution.py:24
  192.3 6.5 %collective-permute-start.42 = (f32[4,1,16]{2,1,0:T(1,128)S(1)}, f32[4,1,16]{2,1,0:T(1,128)S(1)}, u32[]{:S(2)}, u32[]{:S(2)}) collective-permute-start(f32[4,1,16]{2,1,0:T(1,128)S(1)} %get-tuple-element.94), channel_id=1, source_target_pairs={{1,0},{2,1},{3,2},{4,3},{5,4},{6,5},{7,6},{9,8},{10,9},{11,10},{12... | collective-permute-start | bytes 776 | tf_op jit(solution)/shard_map/ppermute | solution.py:26
  193.6 17.8 %collective-permute-start.51 = (f32[3,1,8]{2,1,0:T(1,128)S(1)}, f32[3,1,8]{2,1,0:T(1,128)S(1)}, u32[]{:S(2)}, u32[]{:S(2)}) collective-permute-start(f32[3,1,8]{2,1,0:T(1,128)S(1)} %pad_maximum_fusion.210), channel_id=1, source_target_pairs={{0,1},{1,2},{2,3},{3,4},{4,5},{5,6},{6,7},{8,9},{9,10},{10,11},{11... | collective-permute-start | bytes 296 | tf_op jit(solution)/shard_map/ppermute | solution.py:24
  199.0 6.1 %collective-permute-start.45 = (f32[1,2,16]{2,1,0:T(2,128)S(1)}, f32[1,2,16]{2,1,0:T(2,128)S(1)}, u32[]{:S(2)}, u32[]{:S(2)}) collective-permute-start(f32[1,2,16]{2,1,0:T(2,128)S(1)} %get-tuple-element.102), channel_id=1, source_target_pairs={{0,8},{8,16},{16,24},{1,9},{9,17},{17,25},{2,10},{10,18},{18,26},{... | collective-permute-start | bytes 392 | tf_op jit(solution)/shard_map/ppermute | solution.py:24
  202.4 5.5 %collective-permute-start.44 = (f32[1,2,16]{2,1,0:T(2,128)S(1)}, f32[1,2,16]{2,1,0:T(2,128)S(1)}, u32[]{:S(2)}, u32[]{:S(2)}) collective-permute-start(f32[1,2,16]{2,1,0:T(2,128)S(1)} %get-tuple-element.103), channel_id=1, source_target_pairs={{8,0},{16,8},{24,16},{9,1},{17,9},{25,17},{10,2},{18,10},{26,18},{... | collective-permute-start | bytes 392 | tf_op jit(solution)/shard_map/ppermute | solution.py:26
  203.7 7.7 %collective-permute-start.50 = (f32[3,1,8]{2,1,0:T(1,128)S(1)}, f32[3,1,8]{2,1,0:T(1,128)S(1)}, u32[]{:S(2)}, u32[]{:S(2)}) collective-permute-start(f32[3,1,8]{2,1,0:T(1,128)S(1)} %pad_maximum_fusion.210), channel_id=1, source_target_pairs={{1,0},{2,1},{3,2},{4,3},{5,4},{6,5},{7,6},{9,8},{10,9},{11,10},{12... | collective-permute-start | bytes 296 | tf_op jit(solution)/shard_map/ppermute | solution.py:26
  210.1 5.6 %collective-permute-start.46 = (f32[4,1,16]{2,1,0:T(1,128)S(1)}, f32[4,1,16]{2,1,0:T(1,128)S(1)}, u32[]{:S(2)}, u32[]{:S(2)}) collective-permute-start(f32[4,1,16]{2,1,0:T(1,128)S(1)} %get-tuple-element.92), channel_id=1, source_target_pairs={{1,0},{2,1},{3,2},{4,3},{5,4},{6,5},{7,6},{9,8},{10,9},{11,10},{12... | collective-permute-start | bytes 776 | tf_op jit(solution)/shard_map/ppermute | solution.py:26
  219.0 5.5 %collective-permute-start.52 = (f32[1,1,8]{2,1,0:T(1,128)S(1)}, f32[1,1,8]{2,1,0:T(1,128)S(1)}, u32[]{:S(2)}, u32[]{:S(2)}) collective-permute-start(f32[1,1,8]{2,1,0:T(1,128)S(1)} %get-tuple-element.5), channel_id=1, source_target_pairs={{8,0},{16,8},{24,16},{9,1},{17,9},{25,17},{10,2},{18,10},{26,18},{... | collective-permute-start | bytes 104 | tf_op jit(solution)/shard_map/ppermute | solution.py:26
  227.3 5.9 %collective-permute-start.54 = (f32[3,1,8]{2,1,0:T(1,128)S(1)}, f32[3,1,8]{2,1,0:T(1,128)S(1)}, u32[]{:S(2)}, u32[]{:S(2)}) collective-permute-start(f32[3,1,8]{2,1,0:T(1,128)S(1)} %pad_maximum_fusion.211), channel_id=1, source_target_pairs={{1,0},{2,1},{3,2},{4,3},{5,4},{6,5},{7,6},{9,8},{10,9},{11,10},{12... | collective-permute-start | bytes 296 | tf_op jit(solution)/shard_map/ppermute | solution.py:26
  236.1 5.5 %collective-permute-start.56 = (f32[1,1,8]{2,1,0:T(1,128)S(1)}, f32[1,1,8]{2,1,0:T(1,128)S(1)}, u32[]{:S(2)}, u32[]{:S(2)}) collective-permute-start(f32[1,1,8]{2,1,0:T(1,128)S(1)} %fusion.317), channel_id=1, source_target_pairs={{8,0},{16,8},{24,16},{9,1},{17,9},{25,17},{10,2},{18,10},{26,18},{... | collective-permute-start | bytes 104 | tf_op jit(solution)/shard_map/ppermute | solution.py:26
  244.5 4.9 %collective-permute-start.58 = (f32[3,1,8]{2,1,0:T(1,128)S(1)}, f32[3,1,8]{2,1,0:T(1,128)S(1)}, u32[]{:S(2)}, u32[]{:S(2)}) collective-permute-start(f32[3,1,8]{2,1,0:T(1,128)S(1)} %pad_maximum_fusion.212), channel_id=1, source_target_pairs={{1,0},{2,1},{3,2},{4,3},{5,4},{6,5},{7,6},{9,8},{10,9},{11,10},{12... | collective-permute-start | bytes 296 | tf_op jit(solution)/shard_map/ppermute | solution.py:26
  253.0 5.5 %collective-permute-start.60 = (f32[1,1,8]{2,1,0:T(1,128)S(1)}, f32[1,1,8]{2,1,0:T(1,128)S(1)}, u32[]{:S(2)}, u32[]{:S(2)}) collective-permute-start(f32[1,1,8]{2,1,0:T(1,128)S(1)} %fusion.316), channel_id=1, source_target_pairs={{8,0},{16,8},{24,16},{9,1},{17,9},{25,17},{10,2},{18,10},{26,18},{... | collective-permute-start | bytes 104 | tf_op jit(solution)/shard_map/ppermute | solution.py:26
  261.3 4.9 %collective-permute-start.62 = (f32[3,1,8]{2,1,0:T(1,128)S(1)}, f32[3,1,8]{2,1,0:T(1,128)S(1)}, u32[]{:S(2)}, u32[]{:S(2)}) collective-permute-start(f32[3,1,8]{2,1,0:T(1,128)S(1)} %pad_maximum_fusion.213), channel_id=1, source_target_pairs={{1,0},{2,1},{3,2},{4,3},{5,4},{6,5},{7,6},{9,8},{10,9},{11,10},{12... | collective-permute-start | bytes 296 | tf_op jit(solution)/shard_map/ppermute | solution.py:26
  268.3 5.5 %collective-permute-start.64 = (f32[1,1,8]{2,1,0:T(1,128)S(1)}, f32[1,1,8]{2,1,0:T(1,128)S(1)}, u32[]{:S(2)}, u32[]{:S(2)}) collective-permute-start(f32[1,1,8]{2,1,0:T(1,128)S(1)} %fusion.315), channel_id=1, source_target_pairs={{8,0},{16,8},{24,16},{9,1},{17,9},{25,17},{10,2},{18,10},{26,18},{... | collective-permute-start | bytes 104 | tf_op jit(solution)/shard_map/ppermute | solution.py:26
  283.6 5.5 %collective-permute-start.68 = (f32[1,1,8]{2,1,0:T(1,128)S(1)}, f32[1,1,8]{2,1,0:T(1,128)S(1)}, u32[]{:S(2)}, u32[]{:S(2)}) collective-permute-start(f32[1,1,8]{2,1,0:T(1,128)S(1)} %fusion.314), channel_id=1, source_target_pairs={{8,0},{16,8},{24,16},{9,1},{17,9},{25,17},{10,2},{18,10},{26,18},{... | collective-permute-start | bytes 104 | tf_op jit(solution)/shard_map/ppermute | solution.py:26
  298.9 5.5 %collective-permute-start.72 = (f32[1,1,8]{2,1,0:T(1,128)S(1)}, f32[1,1,8]{2,1,0:T(1,128)S(1)}, u32[]{:S(2)}, u32[]{:S(2)}) collective-permute-start(f32[1,1,8]{2,1,0:T(1,128)S(1)} %fusion.313), channel_id=1, source_target_pairs={{8,0},{16,8},{24,16},{9,1},{17,9},{25,17},{10,2},{18,10},{26,18},{... | collective-permute-start | bytes 104 | tf_op jit(solution)/shard_map/ppermute | solution.py:26
  314.2 5.5 %collective-permute-start.76 = (f32[1,1,8]{2,1,0:T(1,128)S(1)}, f32[1,1,8]{2,1,0:T(1,128)S(1)}, u32[]{:S(2)}, u32[]{:S(2)}) collective-permute-start(f32[1,1,8]{2,1,0:T(1,128)S(1)} %fusion.312), channel_id=1, source_target_pairs={{8,0},{16,8},{24,16},{9,1},{17,9},{25,17},{10,2},{18,10},{26,18},{... | collective-permute-start | bytes 104 | tf_op jit(solution)/shard_map/ppermute | solution.py:26
  329.7 5.5 %collective-permute-start.80 = (f32[1,2,16]{2,1,0:T(2,128)S(1)}, f32[1,2,16]{2,1,0:T(2,128)S(1)}, u32[]{:S(2)}, u32[]{:S(2)}) collective-permute-start(f32[1,2,16]{2,1,0:T(2,128)S(1)} %get-tuple-element.100), channel_id=1, source_target_pairs={{8,0},{16,8},{24,16},{9,1},{17,9},{25,17},{10,2},{18,10},{26,18},{... | collective-permute-start | bytes 392 | tf_op jit(solution)/shard_map/ppermute | solution.py:26
  345.0 5.5 %collective-permute-start.84 = (f32[1,2,16]{2,1,0:T(2,128)S(1)}, f32[1,2,16]{2,1,0:T(2,128)S(1)}, u32[]{:S(2)}, u32[]{:S(2)}) collective-permute-start(f32[1,2,16]{2,1,0:T(2,128)S(1)} %get-tuple-element.98), channel_id=1, source_target_pairs={{8,0},{16,8},{24,16},{9,1},{17,9},{25,17},{10,2},{18,10},{26,18},{... | collective-permute-start | bytes 392 | tf_op jit(solution)/shard_map/ppermute | solution.py:26
  360.6 5.5 %collective-permute-start.88 = (f32[1,4,32]{2,1,0:T(4,128)S(1)}, f32[1,4,32]{2,1,0:T(4,128)S(1)}, u32[]{:S(2)}, u32[]{:S(2)}) collective-permute-start(f32[1,4,32]{2,1,0:T(4,128)S(1)} %get-tuple-element.80), channel_id=1, source_target_pairs={{8,0},{16,8},{24,16},{9,1},{17,9},{25,17},{10,2},{18,10},{26,18},{... | collective-permute-start | bytes 1544 | tf_op jit(solution)/shard_map/ppermute | solution.py:26
  375.9 5.5 %collective-permute-start.92 = (f32[1,4,32]{2,1,0:T(4,128)S(1)}, f32[1,4,32]{2,1,0:T(4,128)S(1)}, u32[]{:S(2)}, u32[]{:S(2)}) collective-permute-start(f32[1,4,32]{2,1,0:T(4,128)S(1)} %get-tuple-element.78), channel_id=1, source_target_pairs={{8,0},{16,8},{24,16},{9,1},{17,9},{25,17},{10,2},{18,10},{26,18},{... | collective-permute-start | bytes 1544 | tf_op jit(solution)/shard_map/ppermute | solution.py:26
  392.2 5.5 %collective-permute-start.96 = (f32[1,8,64]{2,1,0:T(8,128)S(1)}, f32[1,8,64]{2,1,0:T(8,128)S(1)}, u32[]{:S(2)}, u32[]{:S(2)}) collective-permute-start(f32[1,8,64]{2,1,0:T(8,128)S(1)} %get-tuple-element.60), channel_id=1, source_target_pairs={{8,0},{16,8},{24,16},{9,1},{17,9},{25,17},{10,2},{18,10},{26,18},{... | collective-permute-start | bytes 6152 | tf_op jit(solution)/shard_map/ppermute | solution.py:26
  407.6 5.5 %collective-permute-start.100 = (f32[1,8,64]{2,1,0:T(8,128)S(1)}, f32[1,8,64]{2,1,0:T(8,128)S(1)}, u32[]{:S(2)}, u32[]{:S(2)}) collective-permute-start(f32[1,8,64]{2,1,0:T(8,128)S(1)} %get-tuple-element.58), channel_id=1, source_target_pairs={{8,0},{16,8},{24,16},{9,1},{17,9},{25,17},{10,2},{18,10},{26,18},{... | collective-permute-start | bytes 6152 | tf_op jit(solution)/shard_map/ppermute | solution.py:26
  433.9 5.5 %collective-permute-start.104 = (f32[1,16,128]{2,1,0:T(8,128)S(1)}, f32[1,16,128]{2,1,0:T(8,128)S(1)}, u32[]{:S(2)}, u32[]{:S(2)}) collective-permute-start(f32[1,16,128]{2,1,0:T(8,128)S(1)} %get-tuple-element.40), channel_id=1, source_target_pairs={{8,0},{16,8},{24,16},{9,1},{17,9},{25,17},{10,2},{18,10},{26,18},{... | collective-permute-start | bytes 24584 | tf_op jit(solution)/shard_map/ppermute | solution.py:26
  449.7 5.5 %collective-permute-start.108 = (f32[1,16,128]{2,1,0:T(8,128)S(1)}, f32[1,16,128]{2,1,0:T(8,128)S(1)}, u32[]{:S(2)}, u32[]{:S(2)}) collective-permute-start(f32[1,16,128]{2,1,0:T(8,128)S(1)} %get-tuple-element.38), channel_id=1, source_target_pairs={{8,0},{16,8},{24,16},{9,1},{17,9},{25,17},{10,2},{18,10},{26,18},{... | collective-permute-start | bytes 24584 | tf_op jit(solution)/shard_map/ppermute | solution.py:26
  (51 other events, 247.8 us)
where the time goes:
time: 471 us; the launch traced here: 464 us
  starting transfers between devices  257 us (55%)
  waiting for transfers between devices  145 us (31%)
  local copies, waits for them, and re-layouts  36.6 us (8%)
  other arithmetic  23.3 us (5%)
    ppermute x56, starting transfers between devices, with_halo(): lax.ppermute(tail, axis, [(i, (i + 1) % count) for i in range(ends)])  179 us
    ppermute x56, waiting for transfers between devices, with_halo(): lax.ppermute(head, axis, [((i + 1) % count, i) for i in range(ends)])  145 us
    ppermute x56, starting transfers between devices, with_halo(): lax.ppermute(head, axis, [((i + 1) % count, i) for i in range(ends)])  72.5 us
    reshape x4, local copies, waits for them, and re-layouts, coarsen(): field.reshape(depth_x // 2, 2, depth_y // 2, 2, depth_z // 2, 2)  20.7 us
  transfers between devices with their start and end apart: 113, of which 40 were waited for; matrix products, arithmetic and copies ran while one was open for 4% of the time, Pallas kernels for 0%

commit v1 on v0

v1 whole, which is shorter than its diff:
```python
import functools

import jax
import jax.numpy as jnp
from jax import lax
from jax.experimental import pallas as pl
from jax.experimental.pallas import tpu as pltpu
from jax.sharding import PartitionSpec as P

POST = 2
CSWEEPS = 8

air_density = 0.0012
omega_factor = 0.8

F32 = jnp.float32
BF16 = jnp.bfloat16
AXES = ("stream", "trans")

HALO = 12
HB = 10
HD = 11
NEAR = 8
FAR = 4
R0 = 4
ROWS0 = 48
R1 = 8
ROWS1 = 40
SHIFT1 = 10


def params(mib):
    return pltpu.CompilerParams(vmem_limit_bytes=mib << 20)


def lanes(shape):
    return lax.broadcasted_iota(jnp.int32, shape, len(shape) - 1)


def subs(shape):
    return lax.broadcasted_iota(jnp.int32, shape, len(shape) - 2)


def log2(n):
    assert n & (n - 1) == 0
    return n.bit_length() - 1


def up(x, st):
    return pltpu.roll(x, x.shape[-1] - st, x.ndim - 1)


def down(x, st):
    return pltpu.roll(x, st, x.ndim - 1)


def over(lo, hi, fn, limit=64, step=4):
    if hi - lo <= limit:
        for i in range(lo, hi):
            fn(i)
        return
    whole = (hi - lo) // step

    def chunk(k, carry):
        for j in range(step):
            fn(lo + k * step + j)
        return carry

    lax.fori_loop(0, whole, chunk, 0)
    for i in range(lo + whole * step, hi):
        fn(i)


def quotient(scale, den):
    return jnp.where(den > 0.0, scale / den, 0.0)


def setup(rho, faces, w, dg, x0, x1, r0, nr, st, level):
    cx, cy, cp = faces
    scale = 2.0 * 0.25**level
    nz = rho.shape[-1]
    rows = pl.ds(r0, nr)
    lane = lanes((nr, nz))
    first, last = lane < st, lane >= nz - st
    cx[x0 - 1, rows, :] = quotient(scale, rho[x0 - 1, rows, :] + rho[x0, rows, :])

    def plane(i):
        here = rho[i, rows, :]
        fx = quotient(scale, here + rho[i + 1, rows, :])
        cx[i, rows, :] = fx
        cy[i, rows, :] = quotient(scale, here + rho[i, pl.ds(r0 + 1, nr), :])
        fp = quotient(scale, here + jnp.where(last, 0.0, up(here, st)))
        fm = jnp.where(first, quotient(scale, here), down(fp, st))
        cp[i, rows, :] = jnp.where(last, 0.0, fp)
        diag = fx + cx[i - 1, rows, :] + cy[i, rows, :] + cy[i, pl.ds(r0 - 1, nr), :] + fp + fm
        dg[i, rows, :] = diag
        w[i, rows, :] = jnp.where(here > 0.0, omega_factor / diag, 0.0)

    over(x0, x1, plane)


def beside(v, faces, i, r0, nr, st):
    cx, cy, cp = faces
    rows = pl.ds(r0, nr)
    here = v[i, rows, :]
    total = cx[i, rows, :] * v[i + 1, rows, :] + cx[i - 1, rows, :] * v[i - 1, rows, :]
    total = total + cy[i, rows, :] * v[i, pl.ds(r0 + 1, nr), :]
    total = total + cy[i, pl.ds(r0 - 1, nr), :] * v[i, pl.ds(r0 - 1, nr), :]
    fz = cp[i, rows, :]
    total = total + (fz * up(here, st) + down(fz * here, st))
    return here, total


def start(v, b, w, x0, x1, r0, nr):
    rows = pl.ds(r0, nr)

    def plane(i):
        v[i, rows, :] = w[i, rows, :] * b[i, rows, :]

    over(x0, x1, plane)


def swept(v, b, w, faces, i, r0, nr, st):
    rows = pl.ds(r0, nr)
    here, total = beside(v, faces, i, r0, nr, st)
    return (1.0 - omega_factor) * here + w[i, rows, :] * (b[i, rows, :] + total)


def sweep(v, out, b, w, faces, x0, x1, r0, nr, st):
    def plane(i):
        out[i, pl.ds(r0, nr), :] = swept(v, b, w, faces, i, r0, nr, st)

    over(x0, x1, plane)


def residual(v, b, dg, faces, i, r0, nr, st):
    here, total = beside(v, faces, i, r0, nr, st)
    rows = pl.ds(r0, nr)
    return b[i, rows, :] + (total - dg[i, rows, :] * here)


def coarsen(fine, out, tmp, pairs, r0, nr, st, to):
    def pair(a, c):
        total = fine(a) + fine(a + 1)
        even = (lanes(total.shape) // st) % 2 == 0
        total = total + jnp.where(even, up(total, st), down(total, st))
        tmp[c, pl.ds(0, nr), :] = total
        half = nr // 2
        out[c, pl.ds(to, half), :] = 0.125 * (
            tmp[c, pl.ds(0, half, stride=2), :] + tmp[c, pl.ds(1, half, stride=2), :]
        )

    a0, c0, count = pairs
    over(0, count, lambda k: pair(a0 + 2 * k, c0 + k))


def doubled(ref, k, row, value):
    n = value.shape[0]
    ref[k, pl.ds(row, n, stride=2), :] = value
    ref[k, pl.ds(row + 1, n, stride=2), :] = value


def half_tile(a, b, upper):
    top = subs(a.shape) < FAR
    return jnp.where(
        upper,
        jnp.where(top, pltpu.roll(a, FAR, 0), b),
        jnp.where(top, a, pltpu.roll(b, FAR, 0)),
    )


def pack_kernel(groups, rhs, vof, owner, cell, force, dens, xa, xb, ya, yb, disc):
    nx, ny, nz = rhs.shape
    s_even = lax.axis_index("stream") % 2 == 0
    t_even = lax.axis_index("trans") % 2 == 0
    for i in range(nx):
        dens[i] = air_density + ((1.0 - air_density) / 1000.0) * vof[i].astype(F32)
    tail_b, tail_d = nx - HB, nx - HD
    for out, tail in ((xa, s_even), (xb, jnp.logical_not(s_even))):
        at_b, at_d = jnp.where(tail, tail_b, 0), jnp.where(tail, tail_d, 0)
        for i in range(HB):
            out[i] = rhs[at_b + i]
        for i in range(HD):
            out[HB + i] = dens[at_d + i]
    for i in range(nx):
        b, d = rhs[i], dens[i]
        mid_b, mid_d = b[FAR : FAR + 8], d[FAR : FAR + 8]
        for out, tail in ((ya, t_even), (yb, jnp.logical_not(t_even))):
            out[i] = jnp.where(tail, b[ny - NEAR :], b[:NEAR])
            out[nx + i] = jnp.where(tail, d[ny - NEAR :], d[:NEAR])
            out[2 * nx + i] = half_tile(mid_b, mid_d, jnp.logical_not(tail))
    key = (owner[...] * (nx * ny * nz) + cell[...]).astype(F32)
    rows = key.shape[0]
    values = jnp.concatenate([key, force[...]], axis=0)
    if 2 * rows < 8:
        values = jnp.concatenate([values] * (4 // rows), axis=0)
    for g in range(groups * 2 * rows // 8):
        disc[pl.ds(8 * g, 8), :] = values


def corner_kernel(xa, xb, ca, cb):
    ny = xa.shape[1]
    s_even = lax.axis_index("stream") % 2 == 0
    t_even = lax.axis_index("trans") % 2 == 0
    base = 0
    for x, high in ((xa, s_even), (xb, jnp.logical_not(s_even))):
        for i in range(HB + HD):
            tile = x[i]
            low_rows, high_rows = tile[:NEAR], tile[ny - NEAR :]
            ca[base + i] = jnp.where(t_even, high_rows, low_rows)
            cb[base + i] = jnp.where(t_even, low_rows, high_rows)
        at_b = jnp.where(high, 0, HB - FAR)
        at_d = jnp.where(high, HB, HB + HD - FAR)
        for i in range(FAR):
            mid_b = x[at_b + i, pl.ds(FAR, 8), :]
            mid_d = x[at_d + i, pl.ds(FAR, 8), :]
            ca[base + HB + HD + i] = half_tile(mid_b, mid_d, jnp.logical_not(t_even))
            cb[base + HB + HD + i] = half_tile(mid_b, mid_d, t_even)
        base += HB + HD + FAR


def source_kernel(shape, disc, out, hot, val):
    nx, ny, nz = shape
    slabs, groups = lax.axis_size("stream"), lax.axis_size("trans")
    s, t = lax.axis_index("stream"), lax.axis_index("trans")
    per_slab = disc.shape[0] // slabs
    part = per_slab // groups // 2
    wide = ny + 2 * HALO
    depth = lanes((8, nz))[:1]
    for where_, first_x, count, to in ((-1, nx - HB, HB, 0), (0, 0, nx, HB), (1, 0, HB, HB + nx)):
        slab = s + where_

        def fill(slab=slab, first_x=first_x, count=count, to=to):
            base = pl.multiple_of(slab * per_slab, 8)
            cols = part * groups * nz
            zrow = subs((nz, nz))
            mrow = subs((count * wide, nz))
            for g in range(groups):
                for p in range(part):
                    at = (g * part + p) * nz
                    tile = disc[pl.ds(base + (g * 2 * part) // 8 * 8, 8), :]
                    r = (g * 2 * part) % 8 + p
                    key = tile[r : r + 1].astype(jnp.int32)
                    f = tile[r + part : r + part + 1]
                    z = key & (nz - 1)
                    y = (key >> log2(nz)) & (ny - 1)
                    x = (key >> log2(nz * ny)) & (nx - 1)
                    o = key >> log2(nz * ny * nx)
                    row = (o - t) * ny + y + HALO
                    ok = (row >= 0) & (row < wide) & (x >= first_x) & (x < first_x + count)
                    m = jnp.where(ok, (x - first_x) * wide + row, -1)
                    hot[pl.ds(0, count * wide), pl.ds(at, nz)] = (
                        jnp.where(mrow == m, 1.0, 0.0).astype(BF16)
                    )
                    hi = f.astype(BF16).astype(F32)
                    mid = (f - hi).astype(BF16).astype(F32)
                    low = f - hi - mid
                    here = zrow == z
                    for q, piece in enumerate((hi, mid, low)):
                        val[pl.ds(q * nz, nz), pl.ds(at, nz)] = (
                            jnp.where(here, piece, 0.0).astype(BF16)
                        )
            got = lax.dot_general(
                hot[pl.ds(0, count * wide), pl.ds(0, cols)],
                val[:, pl.ds(0, cols)],
                (((1,), (1,)), ((), ())),
                preferred_element_type=F32,
            )
            got = got[:, :nz] + got[:, nz : 2 * nz] + got[:, 2 * nz :]
            for i in range(count):
                out[to + i] = got[i * wide : (i + 1) * wide]

        if where_ == 0:
            fill()
        else:
            inside = slab >= 0 if where_ < 0 else slab < slabs
            pl.when(inside)(fill)

            @pl.when(jnp.logical_not(inside))
            def _(count=count, to=to):
                for i in range(count):
                    out[to + i] = jnp.zeros(out.shape[1:], F32)


def pre_kernel(
    rhs, dens, xa, xb, ya, yb, ca, cb, source,
    slots, v0, b0, w0, cx0, cy0, cp0, v1, b1, w1, cx1, cy1, cp1,
    rho0, dg0, u0, rho1, dg1, u1, tmp0, tmp1,
):
    nx, ny, nz = rhs.shape
    s, t = lax.axis_index("stream"), lax.axis_index("trans")
    groups = lax.axis_size("trans")
    s_even, t_even = s % 2 == 0, t % 2 == 0
    own = R0 + HALO
    full = nx + 2 * HALO
    zero0 = jnp.zeros((ROWS0, nz), F32)
    for i in range(full):
        rho0[i] = zero0
        b0[i] = zero0
    for i in range(nx):
        b0[HALO + i, pl.ds(own, ny), :] = rhs[i]
        rho0[HALO + i, pl.ds(own, ny), :] = dens[i]

    def sides(a, b):
        low = jnp.where(t_even, b, a)
        high = jnp.where(t_even, a, b)
        return jnp.where(t > 0, low, 0.0), jnp.where(t < groups - 1, high, 0.0)

    def near(ref, i, a, b):
        low, high = sides(a, b)
        ref[i, pl.ds(own - NEAR, NEAR), :] = low
        ref[i, pl.ds(own + ny, NEAR), :] = high

    def far(i, a, b):
        low, high = sides(a, b)
        b0[i, pl.ds(own - NEAR - FAR, FAR), :] = low[:FAR]
        b0[i, pl.ds(own + ny + NEAR, FAR), :] = high[:FAR]
        rho0[i, pl.ds(own - NEAR - FAR, FAR), :] = low[FAR:]
        rho0[i, pl.ds(own + ny + NEAR, FAR), :] = high[FAR:]

    for i in range(nx):
        near(b0, HALO + i, ya[i], yb[i])
        near(rho0, HALO + i, ya[nx + i], yb[nx + i])
        far(HALO + i, ya[2 * nx + i], yb[2 * nx + i])
    base = 0
    for x, high in ((xa, s_even), (xb, jnp.logical_not(s_even))):
        at_b = jnp.where(high, HALO + nx, HALO - HB)
        at_d = jnp.where(high, HALO + nx, HALO - HD)
        at_f = jnp.where(high, HALO + nx, HALO - FAR)
        for i in range(HB):
            b0[at_b + i, pl.ds(own, ny), :] = x[i]
            near(b0, at_b + i, ca[base + i], cb[base + i])
        for i in range(HD):
            rho0[at_d + i, pl.ds(own, ny), :] = x[HB + i]
            near(rho0, at_d + i, ca[base + HB + i], cb[base + HB + i])
        for i in range(FAR):
            k = base + HB + HD + i
            far(at_f + i, ca[k], cb[k])
        base += HB + HD + FAR
    wide = ny + 2 * HALO
    for i in range(nx + 2 * HB):
        at = HALO - HB + i
        b0[at, pl.ds(R0, wide), :] = b0[at, pl.ds(R0, wide), :] + source[i]

    f0 = (cx0, cy0, cp0)
    lo, hi = HALO - HB, HALO + nx + HB
    zero_row = jnp.zeros((1, nz), F32)
    for i in range(lo - 1, hi + 1):
        for ref in (u0, v0, cy0):
            ref[i, pl.ds(R0 - 1, 1), :] = zero_row
        for ref in (u0, v0):
            ref[i, pl.ds(R0 + wide, 1), :] = zero_row
    setup(rho0, f0, w0, dg0, lo, hi, R0, wide, 1, 0)
    start(u0, b0, w0, lo, hi, R0, wide)
    sweep(u0, v0, b0, w0, f0, lo + 1, hi - 1, R0, wide, 1)

    half = nx // 2 + HALO
    wide1 = 24
    zero1 = jnp.zeros((ROWS1, nz), F32)
    for i in range(half):
        for ref in (rho1, b1, u1, v1, cy1):
            ref[i] = zero1
    for i in range(half):
        tmp0[i] = zero0

    def rho_rows(i):
        return rho0[i, pl.ds(R0, wide), :]

    rows_to = SHIFT1
    coarsen(rho_rows, rho1, tmp0, (2, 1, half - 2), R0, wide, 1, rows_to)

    def res_rows(i):
        return residual(v0, b0, dg0, f0, i, R0, wide, 1)

    coarsen(res_rows, b1, tmp0, (lo + 2, (lo + 2) // 2, (hi - lo - 4) // 2), R0, wide, 1, rows_to)
    f1 = (cx1, cy1, cp1)
    lo1, hi1 = (lo + 2) // 2, (hi - 2) // 2
    setup(rho1, f1, w1, dg1, lo1, hi1, R1, wide1, 2, 1)
    start(u1, b1, w1, lo1, hi1, R1, wide1)
    sweep(u1, v1, b1, w1, f1, lo1 + 1, hi1 - 1, R1, wide1, 2)

    own1 = SHIFT1 + HALO // 2
    ny1 = ny // 2
    first1 = HALO // 2

    def packed(fine):
        total = None
        for k in range(nx // 4):
            a = first1 + 2 * k
            pairs = fine(a) + fine(a + 1)
            even = (lanes(pairs.shape) // 2) % 2 == 0
            pairs = pairs + jnp.where(even, up(pairs, 2), down(pairs, 2))
            turn = lanes(pairs.shape) % 4 == k
            total = jnp.where(turn, pairs, 0.0 if total is None else total)
        tmp1[...] = total
        return 0.125 * (tmp1[pl.ds(0, ny1 // 2, stride=2), :] + tmp1[pl.ds(1, ny1 // 2, stride=2), :])

    rows2 = ny1 // 2
    slots[0, pl.ds(0, rows2), :] = packed(
        lambda i: residual(v1, b1, dg1, f1, i, own1, ny1, 2)
    )
    slots[0, pl.ds(rows2, rows2), :] = packed(lambda i: rho1[i, pl.ds(own1, ny1), :])
    slot = slots[0]

    def put(g):
        slots[g] = slot

    over(1, slots.shape[0], put)


class Coarse:
    def __init__(self, k, refs, planes, rows, mult, nz):
        self.rho, self.cx, self.cy, self.cp, self.w, self.dg, self.b, self.va, self.vb = refs
        self.planes, self.rows = planes, rows
        self.pitch, self.mult, self.st = 1 << k, mult >> k, mult << k
        self.level = 2 + k
        lane = lanes((rows, nz))
        self.sub = (lane // self.pitch) % self.mult
        self.even_z = (lane // self.st) % 2 == 0
        self.first, self.last = lane < self.st, lane >= nz - self.st
        self.at = pl.ds(8, rows)

    def each(self, fn):
        over(1, 1 + self.planes, fn, 8, 2)

    def next_x(self, here, above):
        if self.mult == 1:
            return above
        far = down(above, (self.mult - 1) * self.pitch)
        return jnp.where(self.sub == self.mult - 1, far, up(here, self.pitch))

    def prev_x(self, here, below):
        if self.mult == 1:
            return below
        far = up(below, (self.mult - 1) * self.pitch)
        return jnp.where(self.sub == 0, far, down(here, self.pitch))

    def setup(self):
        scale = 2.0 * 0.25**self.level
        rho, cx, cy, cp, at, n = self.rho, self.cx, self.cy, self.cp, self.at, self.rows
        cx[0, at, :] = quotient(scale, self.next_x(rho[0, at, :], rho[1, at, :]))

        def plane(i):
            here = rho[i, at, :]
            fx = quotient(scale, here + self.next_x(here, rho[i + 1, at, :]))
            cx[i, at, :] = fx
            cy[i, pl.ds(0, n + 8), :] = quotient(
                scale, rho[i, pl.ds(0, n + 8), :] + rho[i, pl.ds(1, n + 8), :]
            )
            fp = quotient(scale, here + jnp.where(self.last, 0.0, up(here, self.st)))
            fm = jnp.where(self.first, quotient(scale, here), down(fp, self.st))
            cp[i, at, :] = jnp.where(self.last, 0.0, fp)
            diag = fx + self.prev_x(fx, cx[i - 1, at, :]) + fp + fm
            diag = diag + cy[i, at, :] + cy[i, pl.ds(7, n), :]
            self.dg[i, at, :] = diag
            self.w[i, at, :] = omega_factor / diag

        self.each(plane)

    def beside(self, v, i):
        at, n = self.at, self.rows
        here = v[i, at, :]
        fx, fz = self.cx[i, at, :], self.cp[i, at, :]
        total = fx * self.next_x(here, v[i + 1, at, :])
        total = total + self.prev_x(fx * here, self.cx[i - 1, at, :] * v[i - 1, at, :])
        total = total + self.cy[i, at, :] * v[i, pl.ds(9, n), :]
        total = total + self.cy[i, pl.ds(7, n), :] * v[i, pl.ds(7, n), :]
        return here, total + (fz * up(here, self.st) + down(fz * here, self.st))

    def start(self):
        def plane(i):
            self.va[i, self.at, :] = self.w[i, self.at, :] * self.b[i, self.at, :]

        self.each(plane)

    def smooth(self, n):
        for _ in range(n):

            def plane(i):
                here, total = self.beside(self.va, i)
                self.vb[i, self.at, :] = (1.0 - omega_factor) * here + self.w[i, self.at, :] * (
                    self.b[i, self.at, :] + total
                )

            self.each(plane)
            self.va, self.vb = self.vb, self.va

    def residual(self, i):
        here, total = self.beside(self.va, i)
        return self.b[i, self.at, :] + (total - self.dg[i, self.at, :] * here)

    def coarsen(self, fine, out, tmp):
        def plane(i):
            total = fine(i)
            even_x = self.sub % 2 == 0
            total = total + jnp.where(even_x, up(total, self.pitch), down(total, self.pitch))
            total = total + jnp.where(self.even_z, up(total, self.st), down(total, self.st))
            tmp[i, pl.ds(0, self.rows), :] = total
            half = self.rows // 2
            out[i, pl.ds(8, half), :] = 0.125 * (
                tmp[i, pl.ds(0, half, stride=2), :] + tmp[i, pl.ds(1, half, stride=2), :]
            )

        self.each(plane)

    def correct(self, below, tmp):
        def plane(i):
            doubled(tmp, i, 0, below.va[i, below.at, :])
            self.va[i, self.at, :] = self.va[i, self.at, :] + tmp[i, pl.ds(0, self.rows), :]

        self.each(plane)


def post_kernel(slots, v0, b0, w0, cx0, cy0, cp0, v1, b1, w1, cx1, cy1, cp1, out, *refs):
    nx, ny, nz = out.shape
    slabs, groups = lax.axis_size("stream"), lax.axis_size("trans")
    s, t = lax.axis_index("stream"), lax.axis_index("trans")
    gx, gy = nx // 4, ny // 4
    assert gx * (nz // 4) == nz
    rows = groups * gy
    levels = [Coarse(k, refs[9 * k : 9 * k + 9], slabs, rows >> k, gx, nz) for k in range(3)]
    tmp, e1, u1, x1, e0, u0, x0 = refs[27:]
    for c in levels:
        zero = jnp.zeros((c.rows + 16, nz), F32)

        def clear(i, group=(c.rho, c.va, c.vb), zero=zero):
            for ref in group:
                ref[i] = zero

        over(0, slabs + 2, clear)

    two, three, four = levels
    top = subs((8, nz)) < 4

    def unpack(sl):
        for pair in range(groups // 2):
            first = slots[sl * groups + 2 * pair]
            second = slots[sl * groups + 2 * pair + 1]
            to = pl.ds(8 + 8 * pair, 8)
            two.b[1 + sl, to, :] = jnp.where(top, first, pltpu.roll(second, 4, 0))
            two.rho[1 + sl, to, :] = jnp.where(top, pltpu.roll(first, 4, 0), second)

    over(0, slabs, unpack, 8, 2)
    two.setup()
    two.coarsen(lambda i: two.rho[i, two.at, :], three.rho, tmp)
    three.setup()
    three.coarsen(lambda i: three.rho[i, three.at, :], four.rho, tmp)
    four.setup()
    two.start()
    two.smooth(1)
    two.coarsen(two.residual, three.b, tmp)
    three.start()
    three.smooth(1)
    three.coarsen(three.residual, four.b, tmp)
    four.start()
    four.smooth(CSWEEPS - 1)
    three.correct(four, tmp)
    three.smooth(POST)
    two.correct(three, tmp)
    two.smooth(POST)

    f1 = (cx1, cy1, cp1)
    first1, nx1 = HALO // 2, nx // 2
    wide1 = 24
    for i in range(e1.shape[0]):
        e1[i] = jnp.zeros((ROWS1, nz), F32)
    zero_row = jnp.zeros((1, nz), F32)
    for i in range(u1.shape[0]):
        for ref in (u1, x1):
            ref[i, pl.ds(R1 - 1, 1), :] = zero_row
            ref[i, pl.ds(R1 + wide1, 1), :] = zero_row
    place = lanes((gy + 4, nz)) % gx
    around = [two.va[s + k, pl.ds(t * gy + 6, gy + 4), :] for k in range(3)]
    for k in range(gx + 4):
        plane, sub = around[(k + gx - 2) // gx], (k + gx - 2) % gx
        value = plane if sub == 0 else pltpu.roll(plane, nz - sub, 1)
        for m in range(1, gx):
            value = jnp.where(place == m, pltpu.roll(plane, (m - sub) % nz, 1) if m != sub else plane, value)
        doubled(e1, k, SHIFT1 + first1 - 4, value)
    rows1 = pl.ds(R1, wide1)
    for i in range(first1 - 3, first1 + nx1 + 3):
        u1[i, rows1, :] = v1[i, rows1, :] + e1[(i - first1 + 4) // 2, rows1, :]
    sweep(u1, x1, b1, w1, f1, first1 - 2, first1 + nx1 + 2, R1, wide1, 2)
    sweep(x1, u1, b1, w1, f1, first1 - 1, first1 + nx1 + 1, R1, wide1, 2)

    f0 = (cx0, cy0, cp0)
    own = R0 + HALO
    low, count = own - 8, ny + 16
    for k in range(nx1 + 2):
        value = u1[first1 - 1 + k, pl.ds(SHIFT1 + first1 - 4, ny // 2 + 8), :]
        doubled(e0, k, low, value)
    for i in range(HALO - 2, HALO + nx + 2):
        rows0 = pl.ds(low, count)
        u0[i, rows0, :] = v0[i, rows0, :] + e0[(i - HALO + 2) // 2, rows0, :]
    sweep(u0, x0, b0, w0, f0, HALO - 1, HALO + nx + 1, low + 7, count - 8, 1)
    for i in range(nx):
        out[i] = swept(x0, b0, w0, f0, HALO + i, own, ny, 1)


def exchange(count, other, parity, open_ends):
    pairs = []
    for i in range(count):
        j = ((i + parity) ^ 1) - parity
        if 0 <= j < count:
            pairs.append((i, j))
        elif not open_ends:
            pairs.append((i, count - 1 - i))
    return pairs


def swap(value, axis, parity, open_ends):
    count = lax.axis_size(axis)
    return lax.ppermute(value, axis, exchange(count, None, parity, open_ends))


def sds(*shape):
    return jax.ShapeDtypeStruct(shape, F32)


def body(rhs, vof, disc_owner, disc_cell, disc_force):
    nx, ny, nz = rhs.shape
    slabs, groups = lax.axis_size("stream"), lax.axis_size("trans")
    devices = slabs * groups
    rows = disc_cell.shape[1] // nz
    wide = ny + 2 * HALO
    halo_x = sds(HB + HD, ny, nz)
    halo_y = sds(3 * nx, 8, nz)
    corner = sds(2 * (HB + HD + FAR), 8, nz)

    dens, xa, xb, ya, yb, disc = pl.pallas_call(
        functools.partial(pack_kernel, devices),
        out_shape=(sds(nx, ny, nz), halo_x, halo_x, halo_y, halo_y, sds(devices * 2 * rows, nz)),
        compiler_params=params(12),
        name="pack",
    )(
        rhs,
        vof,
        disc_owner.reshape(rows, nz),
        disc_cell.reshape(rows, nz),
        disc_force.reshape(rows, nz),
    )
    disc = lax.all_to_all(disc, AXES, 0, 0, tiled=True)
    xa = swap(xa, "stream", 0, True)
    xb = swap(xb, "stream", 1, True)
    ya = swap(ya, "trans", 0, False)
    yb = swap(yb, "trans", 1, False)
    ca, cb = pl.pallas_call(
        corner_kernel, out_shape=(corner, corner), compiler_params=params(8), name="corner"
    )(xa, xb)
    ca = swap(ca, "trans", 0, False)
    cb = swap(cb, "trans", 1, False)
    cols = groups * rows * nz
    source = pl.pallas_call(
        functools.partial(source_kernel, (nx, ny, nz)),
        out_shape=sds(nx + 2 * HB, wide, nz),
        scratch_shapes=[pltpu.VMEM((nx * wide, cols), BF16), pltpu.VMEM((3 * nz, cols), BF16)],
        compiler_params=params(24),
        name="source",
    )(disc)
    full, half = nx + 2 * HALO, nx // 2 + HALO
    frame0, frame1 = sds(full, ROWS0, nz), sds(half, ROWS1, nz)
    s0, s1 = pltpu.VMEM(frame0.shape, F32), pltpu.VMEM(frame1.shape, F32)
    slots, *state = pl.pallas_call(
        pre_kernel,
        out_shape=(sds(devices, 8, nz), *([frame0] * 6), *([frame1] * 6)),
        scratch_shapes=[
            s0, s0, s0, s1, s1, s1,
            pltpu.VMEM((half, ROWS0, nz), F32), pltpu.VMEM((ny // 2, nz), F32),
        ],
        compiler_params=params(28),
        name="presmooth",
    )(rhs, dens, xa, xb, ya, yb, ca, cb, source)
    slots = lax.all_to_all(slots, AXES, 0, 0, tiled=True)
    gy = groups * ny // 4
    scratch = [pltpu.VMEM((slabs + 2, (gy >> k) + 16, nz), F32) for k in range(3) for _ in range(9)]
    scratch += [
        pltpu.VMEM((slabs + 2, gy, nz), F32),
        pltpu.VMEM((nx // 4 + 4, ROWS1, nz), F32),
        s1,
        s1,
        pltpu.VMEM((nx // 2 + 2, ROWS0, nz), F32),
        s0,
        s0,
    ]
    return pl.pallas_call(
        post_kernel,
        out_shape=sds(nx, ny, nz),
        scratch_shapes=scratch,
        compiler_params=params(28),
        name="postsmooth",
    )(slots, *state)


def solution(mesh):
    return jax.shard_map(
        body,
        mesh=mesh,
        in_specs=(
            P("stream", "trans", None),
            P("stream", "trans", None),
            P("stream", "trans", None),
            P("stream", "trans"),
            P("stream", "trans"),
        ),
        out_specs=P("stream", "trans", None),
        check_vma=False,
    )
```

time: 471 us -> 53.6 us (0.11); the launches traced: 464 us -> 53.4 us
  starting transfers between devices: 257 us -> 7.21 us
  waiting for transfers between devices: 145 us -> 3.72 us
  local copies, waits for them, and re-layouts: 36.6 us -> 2.52 us
  blocking collectives: 0 us -> 26.5 us
  other arithmetic: 23.3 us -> 0 us
  Pallas kernels: 0 us -> 13.4 us
    ppermute x112 -> x6, starting transfers between devices: 252 us -> 7.21 us  [swap(): return lax.ppermute(value, axis, exchange(count, None, parity, open_ends))]
    ppermute x112 -> x6, waiting for transfers between devices: 145 us -> 3.72 us  [swap(): return lax.ppermute(value, axis, exchange(count, None, parity, open_ends))]
    reshape x8 -> x0, local copies, waits for them, and re-layouts: 29.1 us -> none  [the longest x4 20.7 us: coarsen(): field.reshape(depth_x // 2, 2, depth_y // 2, 2, depth_z // 2, 2)]
    all_to_all x0 -> x2, blocking collectives: none -> 26.5 us  [the longest x1 14.8 us: body(): disc = lax.all_to_all(disc, AXES, 0, 0, tiled=True)]
    pallas_call x0 -> x5, Pallas kernels: none -> 13.4 us  [the longest x1 5.72 us: body(): pl.pallas_call(pre_kernel, out_shape=(sds(devices, 8, nz), *[frame0] * 6,...]
    reduce_sum x10 -> x0, other arithmetic: 9.65 us -> none  [the longest x9 8.88 us: coarsen(): field.reshape(depth_x // 2, 2, depth_y // 2, 2, depth_z // 2, 2)]
    all_to_all x1 -> x0, starting transfers between devices: 5.2 us -> none  [body(): lax.all_to_all(packed.reshape(2, groups, CAP), 'trans', split_axis=1, con...]
  transfers between devices with their start and end apart: 113 -> 6, of which waited for: 40 -> 1; matrix products, arithmetic and copies ran while one was open for 4% -> 0% of each run, Pallas kernels for 0% -> 6%
where the time goes in v1:
time: 53.6 us; the launch traced here: 53.4 us
  blocking collectives  26.5 us (49%)
  Pallas kernels  13.4 us (25%)
  starting transfers between devices  7.21 us (13%)
  waiting for transfers between devices  3.72 us (7%)
  local copies, waits for them, and re-layouts  2.52 us (5%)
    all_to_all x1, blocking collectives, body(): disc = lax.all_to_all(disc, AXES, 0, 0, tiled=True)  14.8 us
    all_to_all x1, blocking collectives, body(): slots = lax.all_to_all(slots, AXES, 0, 0, tiled=True)  11.7 us
    ppermute x6, starting transfers between devices, swap(): return lax.ppermute(value, axis, exchange(count, None, parity, open_ends))  7.21 us
    pallas_call x1, Pallas kernels, body(): pl.pallas_call(pre_kernel, out_shape=(sds(devices, 8, nz), *[frame0] * 6,...  5.72 us
    pallas_call x1, Pallas kernels, body(): pl.pallas_call(post_kernel, out_shape=sds(nx, ny, nz), scratch_shapes=scr...  4.38 us
    ppermute x6, waiting for transfers between devices, swap(): return lax.ppermute(value, axis, exchange(count, None, parity, open_ends))  3.72 us
    pallas_call x1, Pallas kernels, body(): pl.pallas_call(functools.partial(source_kernel, (nx, ny, nz)), out_shape=...  3.15 us
    unnamed x12, local copies, waits for them, and re-layouts  2.52 us
  transfers between devices with their start and end apart: 6, of which 1 were waited for; matrix products, arithmetic and copies ran while one was open for 0% of the time, Pallas kernels for 6%

profile of v1, /device:TPU:0, one launch (start us, length us, event | category | flops | bytes accessed | tf_op | source)
XLA Modules:
  0.0 53.4 jit_solution(10139494814988740964)
XLA Ops:
  0.0 0.0 copy-start.4
  0.0 0.0 copy-start.5
  0.0 0.0 copy-start.3
  0.0 0.7 %copy-done.4 = s32[1,256]{1,0:T(1,128)S(1)} copy-done((s32[1,256]{1,0:T(1,128)S(1)}, s32[1,256]{1,0:T(1,128)}, u32[]{:S(2)}) %copy-start.4) | copy-done | bytes 1048
  0.7 0.0 copy-done.5
  0.7 0.0 copy-done.3
  0.7 0.0 copy-start
  0.7 0.9 %copy-done = f32[16,16,128]{2,1,0:T(8,128)S(1)} copy-done((f32[16,16,128]{2,1,0:T(8,128)S(1)}, f32[16,16,128]{2,1,0:T(8,128)}, u32[]{:S(2)}) %copy-start) | copy-done | bytes 131096
  1.6 0.0 copy-start.2
  1.6 0.9 %copy-done.2 = s32[16,16,128]{2,1,0:T(8,128)S(1)} copy-done((s32[16,16,128]{2,1,0:T(8,128)S(1)}, s32[16,16,128]{2,1,0:T(8,128)}, u32[]{:S(2)}) %copy-start.2) | copy-done | bytes 131096
  2.5 0.1 pack.1
  2.6 3.1 %collective-permute-start = (f32[21,16,128]{2,1,0:T(8,128)S(1)}, f32[21,16,128]{2,1,0:T(8,128)S(1)}, u32[]{:S(2)}, u32[]{:S(2)}) collective-permute-start(f32[21,16,128]{2,1,0:T(8,128)S(1)} %get-tuple-element.27), channel_id=1, source_target_pairs={{0,8},{8,0},{16,24},{24,16},{1,9},{9,1},{17,25},{25,17},{2,10},{10... | collective-permute-start | bytes 516104 | tf_op jit(solution)/shard_map/ppermute | solution.py:613
  5.7 0.7 %collective-permute-start.1 = (f32[21,16,128]{2,1,0:T(8,128)S(1)}, f32[21,16,128]{2,1,0:T(8,128)S(1)}, u32[]{:S(2)}, u32[]{:S(2)}) collective-permute-start(f32[21,16,128]{2,1,0:T(8,128)S(1)} %get-tuple-element.28), channel_id=1, source_target_pairs={{8,16},{16,8},{9,17},{17,9},{10,18},{18,10},{11,19},{19,11},{12,20... | collective-permute-start | bytes 516104 | tf_op jit(solution)/shard_map/ppermute | solution.py:613
  6.4 3.7 %collective-permute-done.xa = f32[21,16,128]{2,1,0:T(8,128)S(1)} collective-permute-done((f32[21,16,128]{2,1,0:T(8,128)S(1)}, f32[21,16,128]{2,1,0:T(8,128)S(1)}, u32[]{:S(2)}, u32[]{:S(2)}) %collective-permute-start) | collective-permute-done | bytes 172064 | tf_op jit(solution)/shard_map/ppermute | solution.py:613
  10.1 0.0 collective-permute-done.1.xb
  10.1 0.1 collective-permute-start.4
  10.2 2.7 %collective-permute-start.5 = (f32[50,8,128]{2,1,0:T(8,128)S(1)}, f32[50,8,128]{2,1,0:T(8,128)S(1)}, u32[]{:S(2)}, u32[]{:S(2)}) collective-permute-start(f32[50,8,128]{2,1,0:T(8,128)S(1)} %get-tuple-element.32), channel_id=1, source_target_pairs={{0,7},{1,2},{2,1},{3,4},{4,3},{5,6},{6,5},{7,0},{8,15},{9,10},{10,... | collective-permute-start | bytes 614408 | tf_op jit(solution)/shard_map/ppermute | solution.py:613
  12.9 0.0 collective-permute-start.2
  12.9 0.6 %collective-permute-start.3 = (f32[48,8,128]{2,1,0:T(8,128)S(1)}, f32[48,8,128]{2,1,0:T(8,128)S(1)}, u32[]{:S(2)}, u32[]{:S(2)}) collective-permute-start(f32[48,8,128]{2,1,0:T(8,128)S(1)} %get-tuple-element.30), channel_id=1, source_target_pairs={{0,7},{1,2},{2,1},{3,4},{4,3},{5,6},{6,5},{7,0},{8,15},{9,10},{10,... | collective-permute-start | bytes 589832 | tf_op jit(solution)/shard_map/ppermute | solution.py:613
  13.6 14.8 %all_to_all.16 = f32[32,4,128]{2,1,0:T(4,128)S(1)} all-to-all(f32[32,4,128]{2,1,0:T(4,128)S(1)} %bitcast.6), channel_id=1, replica_groups=mesh['stream'=4,'trans'=8] {'stream','trans'}, dimensions={0} | all-to-all | bytes 131072 | tf_op jit(solution)/shard_map/all_to_all | solution.py:642
  28.4 0.0 copy-start.1
  28.4 3.2 %source.1 = f32[36,40,128]{2,1,0:T(8,128)S(1)} custom-call(f32[128,128]{1,0:T(8,128)S(1)} %bitcast.5), custom_call_target="tpu_custom_call" | custom-call | tf_op jit(solution)/shard_map/source/pallas_call | solution.py:653
  31.5 0.0 collective-permute-done.2.ya
  31.5 0.0 collective-permute-done.3.yb
  31.5 0.0 collective-permute-done.4.ca
  31.5 0.0 collective-permute-done.5.cb
  31.6 0.0 copy-done.1
  31.6 5.7 %presmooth.1 = (f32[32,8,128]{2,1,0:T(8,128)S(1)}, f32[40,48,128]{2,1,0:T(8,128)S(1)}, f32[40,48,128]{2,1,0:T(8,128)S(1)}, f32[40,48,128]{2,1,0:T(8,128)S(1)}, f...) custom-call(f32[16,16,128]{2,1,0:T(8,128)S(1)} %copy-done.1, ...), custom_call_target="tpu_custom_call" | custom-call | tf_op jit(solution)/shard_map/presmooth/pallas_call | solution.py:663
  37.3 11.7 %all_to_all.17.slots = f32[32,8,128]{2,1,0:T(8,128)S(1)} all-to-all(f32[32,8,128]{2,1,0:T(8,128)S(1)} %get-tuple-element.34), channel_id=1, replica_groups=mesh['stream'=4,'trans'=8] {'stream','trans'}, dimensions={0} | all-to-all | bytes 262144 | tf_op jit(solution)/shard_map/all_to_all | solution.py:673
  49.0 4.4 %postsmooth.1 = f32[16,16,128]{2,1,0:T(8,128)} custom-call(f32[32,8,128]{2,1,0:T(8,128)S(1)} %all_to_all.17.slots, f32[40,48,128]{2,1,0:T(8,128)S(1)} %get-tuple-element.35.v0, f32[40,48,128]{2,1,0:T(8,128)S(1)} %get-tuple-element.36.b0, f32[40,48,128]{2,1,0:T(8,128)S(1)} %get-tuple-element.37.w0, f32[40,48,128]{2,1,0:T(8,128)S(1)} %get-tuple-element.38.cx0, ...), custom_call_target="tpu_custom_call" | custom-call | tf_op jit(solution)/shard_map/postsmooth/pallas_call | solution.py:685
  (1 shorter events, 0.0 us)
Async XLA Ops:
  0.0 0.7 %copy-start.4 = (s32[1,256]{1,0:T(1,128)S(1)}, s32[1,256]{1,0:T(1,128)}, u32[]{:S(2)}) copy-start(s32[1,256]{1,0:T(1,128)} %param.8) | copy-start | bytes 3076
  0.0 0.7 %copy-start.5 = (f32[1,256]{1,0:T(1,128)S(1)}, f32[1,256]{1,0:T(1,128)}, u32[]{:S(2)}) copy-start(f32[1,256]{1,0:T(1,128)} %param.9) | copy-start | bytes 3076
  0.0 0.7 %copy-start.3 = (s32[1,256,1]{1,2,0:T(1,128)S(1)}, s32[1,256,1]{1,2,0:T(1,128)}, u32[]{:S(2)}) copy-start(s32[1,256,1]{1,2,0:T(1,128)} %param.7) | copy-start | bytes 3076
  0.7 0.9 %copy-start = (f32[16,16,128]{2,1,0:T(8,128)S(1)}, f32[16,16,128]{2,1,0:T(8,128)}, u32[]{:S(2)}) copy-start(f32[16,16,128]{2,1,0:T(8,128)} %rhs.3) | copy-start | bytes 393220
  1.6 0.9 %copy-start.2 = (s32[16,16,128]{2,1,0:T(8,128)S(1)}, s32[16,16,128]{2,1,0:T(8,128)}, u32[]{:S(2)}) copy-start(s32[16,16,128]{2,1,0:T(8,128)} %vof.1) | copy-start | bytes 393220
  2.6 7.5 %collective-permute-start = (f32[21,16,128]{2,1,0:T(8,128)S(1)}, f32[21,16,128]{2,1,0:T(8,128)S(1)}, u32[]{:S(2)}, u32[]{:S(2)}) collective-permute-start(f32[21,16,128]{2,1,0:T(8,128)S(1)} %get-tuple-element.27), channel_id=1, source_target_pairs={{0,8},{8,0},{16,24},{24,16},{1,9},{9,1},{17,25},{25,17},{2,10},{10... | collective-permute-start | bytes 516104 | tf_op jit(solution)/shard_map/ppermute | solution.py:613
  5.7 4.4 %collective-permute-start.1 = (f32[21,16,128]{2,1,0:T(8,128)S(1)}, f32[21,16,128]{2,1,0:T(8,128)S(1)}, u32[]{:S(2)}, u32[]{:S(2)}) collective-permute-start(f32[21,16,128]{2,1,0:T(8,128)S(1)} %get-tuple-element.28), channel_id=1, source_target_pairs={{8,16},{16,8},{9,17},{17,9},{10,18},{18,10},{11,19},{19,11},{12,20... | collective-permute-start | bytes 516104 | tf_op jit(solution)/shard_map/ppermute | solution.py:613
  10.1 21.4 %collective-permute-start.4 = (f32[50,8,128]{2,1,0:T(8,128)S(1)}, f32[50,8,128]{2,1,0:T(8,128)S(1)}, u32[]{:S(2)}, u32[]{:S(2)}) collective-permute-start(f32[50,8,128]{2,1,0:T(8,128)S(1)} %get-tuple-element.31), channel_id=1, source_target_pairs={{0,1},{1,0},{2,3},{3,2},{4,5},{5,4},{6,7},{7,6},{8,9},{9,8},{10,11... | collective-permute-start | bytes 614408 | tf_op jit(solution)/shard_map/ppermute | solution.py:613
  10.2 21.3 %collective-permute-start.5 = (f32[50,8,128]{2,1,0:T(8,128)S(1)}, f32[50,8,128]{2,1,0:T(8,128)S(1)}, u32[]{:S(2)}, u32[]{:S(2)}) collective-permute-start(f32[50,8,128]{2,1,0:T(8,128)S(1)} %get-tuple-element.32), channel_id=1, source_target_pairs={{0,7},{1,2},{2,1},{3,4},{4,3},{5,6},{6,5},{7,0},{8,15},{9,10},{10,... | collective-permute-start | bytes 614408 | tf_op jit(solution)/shard_map/ppermute | solution.py:613
  12.9 18.6 %collective-permute-start.2 = (f32[48,8,128]{2,1,0:T(8,128)S(1)}, f32[48,8,128]{2,1,0:T(8,128)S(1)}, u32[]{:S(2)}, u32[]{:S(2)}) collective-permute-start(f32[48,8,128]{2,1,0:T(8,128)S(1)} %get-tuple-element.29), channel_id=1, source_target_pairs={{0,1},{1,0},{2,3},{3,2},{4,5},{5,4},{6,7},{7,6},{8,9},{9,8},{10,11... | collective-permute-start | bytes 589832 | tf_op jit(solution)/shard_map/ppermute | solution.py:613
  12.9 18.6 %collective-permute-start.3 = (f32[48,8,128]{2,1,0:T(8,128)S(1)}, f32[48,8,128]{2,1,0:T(8,128)S(1)}, u32[]{:S(2)}, u32[]{:S(2)}) collective-permute-start(f32[48,8,128]{2,1,0:T(8,128)S(1)} %get-tuple-element.30), channel_id=1, source_target_pairs={{0,7},{1,2},{2,1},{3,4},{4,3},{5,6},{6,5},{7,0},{8,15},{9,10},{10,... | collective-permute-start | bytes 589832 | tf_op jit(solution)/shard_map/ppermute | solution.py:613
  28.4 3.2 %copy-start.1 = (f32[16,16,128]{2,1,0:T(8,128)S(1)}, f32[16,16,128]{2,1,0:T(8,128)}, u32[]{:S(2)}) copy-start(f32[16,16,128]{2,1,0:T(8,128)} %rhs.3) | copy-start | bytes 393220

commit v2 on v1

--- a/solution.py
+++ b/solution.py
@@ -6,6 +6,7 @@
 from jax.experimental import pallas as pl
 from jax.experimental.pallas import tpu as pltpu
 from jax.sharding import PartitionSpec as P
+
 
 POST = 2
 CSWEEPS = 8
@@ -139,7 +140,7 @@
     return b[i, rows, :] + (total - dg[i, rows, :] * here)
 
 
-def coarsen(fine, out, tmp, pairs, r0, nr, st, to):
+def coarsen(fine, out, tmp, pairs, nr, st, to):
     def pair(a, c):
         total = fine(a) + fine(a + 1)
         even = (lanes(total.shape) // st) % 2 == 0
@@ -169,7 +170,17 @@
     )
 
 
-def pack_kernel(groups, rhs, vof, owner, cell, force, dens, xa, xb, ya, yb, disc):
+def pack_kernel(groups, *refs):
+    outside, (rhs, dens, xa, xb, ya, yb, disc) = refs[:5], refs[5:12]
+    vof, owner, cell, force, sems = refs[12:]
+    inside = (rhs, vof, owner, cell, force)
+    copies = [
+        pltpu.make_async_copy(a, b, sems.at[i]) for i, (a, b) in enumerate(zip(outside, inside))
+    ]
+    for copy in copies:
+        copy.start()
+    for copy in copies:
+        copy.wait()
     nx, ny, nz = rhs.shape
     s_even = lax.axis_index("stream") % 2 == 0
     t_even = lax.axis_index("trans") % 2 == 0
@@ -367,12 +378,12 @@
         return rho0[i, pl.ds(R0, wide), :]
 
     rows_to = SHIFT1
-    coarsen(rho_rows, rho1, tmp0, (2, 1, half - 2), R0, wide, 1, rows_to)
+    coarsen(rho_rows, rho1, tmp0, (2, 1, half - 2), wide, 1, rows_to)
 
     def res_rows(i):
         return residual(v0, b0, dg0, f0, i, R0, wide, 1)
 
-    coarsen(res_rows, b1, tmp0, (lo + 2, (lo + 2) // 2, (hi - lo - 4) // 2), R0, wide, 1, rows_to)
+    coarsen(res_rows, b1, tmp0, (lo + 2, (lo + 2) // 2, (hi - lo - 4) // 2), wide, 1, rows_to)
     f1 = (cx1, cy1, cp1)
     lo1, hi1 = (lo + 2) // 2, (hi - 2) // 2
     setup(rho1, f1, w1, dg1, lo1, hi1, R1, wide1, 2, 1)
@@ -597,7 +608,7 @@
         out[i] = swept(x0, b0, w0, f0, HALO + i, own, ny, 1)
 
 
-def exchange(count, other, parity, open_ends):
+def exchange(count, parity, open_ends):
     pairs = []
     for i in range(count):
         j = ((i + parity) ^ 1) - parity
@@ -610,7 +621,11 @@
 
 def swap(value, axis, parity, open_ends):
     count = lax.axis_size(axis)
-    return lax.ppermute(value, axis, exchange(count, None, parity, open_ends))
+    return lax.ppermute(value, axis, exchange(count, parity, open_ends))
+
+
+def gather(value):
+    return lax.all_to_all(value, AXES, 0, 0, tiled=True)
 
 
 def sds(*shape):
@@ -627,19 +642,33 @@
     halo_y = sds(3 * nx, 8, nz)
     corner = sds(2 * (HB + HD + FAR), 8, nz)
 
-    dens, xa, xb, ya, yb, disc = pl.pallas_call(
+    block, row = sds(nx, ny, nz), pltpu.VMEM((rows, nz), jnp.int32)
+    rhs, dens, xa, xb, ya, yb, disc = pl.pallas_call(
         functools.partial(pack_kernel, devices),
-        out_shape=(sds(nx, ny, nz), halo_x, halo_x, halo_y, halo_y, sds(devices * 2 * rows, nz)),
+        out_shape=(block, block, halo_x, halo_x, halo_y, halo_y, sds(devices * 2 * rows, nz)),
+        in_specs=[pl.BlockSpec(memory_space=pltpu.MemorySpace.HBM)] * 5,
+        scratch_shapes=[
+            pltpu.VMEM((nx, ny, nz), jnp.int32),
+            row,
+            row,
+            pltpu.VMEM((rows, nz), F32),
+            pltpu.SemaphoreType.DMA((5,)),
+        ],
         compiler_params=params(12),
         name="pack",
     )(
-        rhs,
-        vof,
-        disc_owner.reshape(rows, nz),
-        disc_cell.reshape(rows, nz),
-        disc_force.reshape(rows, nz),
+        *(
+            pltpu.with_memory_space_constraint(x, pltpu.MemorySpace.HBM)
+            for x in (
+                rhs,
+                vof,
+                disc_owner.reshape(rows, nz),
+                disc_cell.reshape(rows, nz),
+                disc_force.reshape(rows, nz),
+            )
+        )
     )
-    disc = lax.all_to_all(disc, AXES, 0, 0, tiled=True)
+    disc = gather(disc)
     xa = swap(xa, "stream", 0, True)
     xb = swap(xb, "stream", 1, True)
     ya = swap(ya, "trans", 0, False)
@@ -653,7 +682,10 @@
     source = pl.pallas_call(
         functools.partial(source_kernel, (nx, ny, nz)),
         out_shape=sds(nx + 2 * HB, wide, nz),
-        scratch_shapes=[pltpu.VMEM((nx * wide, cols), BF16), pltpu.VMEM((3 * nz, cols), BF16)],
+        scratch_shapes=[
+            pltpu.VMEM((nx * wide, cols), BF16),
+            pltpu.VMEM((3 * nz, cols), BF16),
+        ],
         compiler_params=params(24),
         name="source",
     )(disc)
@@ -670,7 +702,7 @@
         compiler_params=params(28),
         name="presmooth",
     )(rhs, dens, xa, xb, ya, yb, ca, cb, source)
-    slots = lax.all_to_all(slots, AXES, 0, 0, tiled=True)
+    slots = gather(slots)
     gy = groups * ny // 4
     scratch = [pltpu.VMEM((slabs + 2, (gy >> k) + 16, nz), F32) for k in range(3) for _ in range(9)]
     scratch += [

time: 53.6 us -> 52.1 us (0.972)
  local copies, waits for them, and re-layouts: 2.52 us -> 0 us
  Pallas kernels: 13.4 us -> 14.4 us
    unnamed x12 -> x0, local copies, waits for them, and re-layouts: 2.52 us -> none
    pallas_call x1, Pallas kernels: 0.08 us -> 1.09 us  [body(): pl.pallas_call(functools.partial(pack_kernel, devices), out_shape=(block,...]
where the time goes in v2:
time: 52.1 us; the launch traced here: 51.9 us
  blocking collectives  26.5 us (51%)
  Pallas kernels  14.4 us (28%)
  starting transfers between devices  7.21 us (14%)
  waiting for transfers between devices  3.72 us (7%)
    all_to_all x2, blocking collectives, gather(): return lax.all_to_all(value, AXES, 0, 0, tiled=True)  26.5 us
    ppermute x6, starting transfers between devices, swap(): return lax.ppermute(value, axis, exchange(count, parity, open_ends))  7.21 us
    pallas_call x1, Pallas kernels, body(): pl.pallas_call(pre_kernel, out_shape=(sds(devices, 8, nz), *[frame0] * 6,...  5.72 us
    pallas_call x1, Pallas kernels, body(): pl.pallas_call(post_kernel, out_shape=sds(nx, ny, nz), scratch_shapes=scr...  4.38 us
    ppermute x6, waiting for transfers between devices, swap(): return lax.ppermute(value, axis, exchange(count, parity, open_ends))  3.72 us
    pallas_call x1, Pallas kernels, body(): pl.pallas_call(functools.partial(source_kernel, (nx, ny, nz)), out_shape=...  3.15 us
    pallas_call x1, Pallas kernels, body(): pl.pallas_call(functools.partial(pack_kernel, devices), out_shape=(block,...  1.09 us
  transfers between devices with their start and end apart: 6, of which 1 were waited for; matrix products, arithmetic and copies ran while one was open for 0% of the time, Pallas kernels for 6%

profile of v2, /device:TPU:0, one launch (start us, length us, event | category | flops | bytes accessed | tf_op | source)
XLA Modules:
  0.0 51.9 jit_solution(3843511069134428994)
XLA Ops:
  0.0 1.1 %pack.1 = (f32[16,16,128]{2,1,0:T(8,128)S(1)}, f32[16,16,128]{2,1,0:T(8,128)S(1)}, f32[21,16,128]{2,1,0:T(8,128)S(1)}, f32[21,16,128]{2,1,0:T(8,128)S(1)}, f32[4...) custom-call(f32[16,16,128]{2,1,0:T(8,128)} %refs_0_.1, s32[16,16,128]{2,1,0:T(8,128)} %refs_1_.1, ...), custom_call_target="tpu_custom_call" | custom-call | tf_op jit(solution)/shard_map/pack/pallas_call | solution.py:646
  1.1 3.1 %collective-permute-start = (f32[21,16,128]{2,1,0:T(8,128)S(1)}, f32[21,16,128]{2,1,0:T(8,128)S(1)}, u32[]{:S(2)}, u32[]{:S(2)}) collective-permute-start(f32[21,16,128]{2,1,0:T(8,128)S(1)} %get-tuple-element.29), channel_id=1, source_target_pairs={{0,8},{8,0},{16,24},{24,16},{1,9},{9,1},{17,25},{25,17},{2,10},{10... | collective-permute-start | bytes 516104 | tf_op jit(solution)/shard_map/ppermute | solution.py:624
  4.2 0.7 %collective-permute-start.1 = (f32[21,16,128]{2,1,0:T(8,128)S(1)}, f32[21,16,128]{2,1,0:T(8,128)S(1)}, u32[]{:S(2)}, u32[]{:S(2)}) collective-permute-start(f32[21,16,128]{2,1,0:T(8,128)S(1)} %get-tuple-element.30), channel_id=1, source_target_pairs={{8,16},{16,8},{9,17},{17,9},{10,18},{18,10},{11,19},{19,11},{12,20... | collective-permute-start | bytes 516104 | tf_op jit(solution)/shard_map/ppermute | solution.py:624
  4.9 3.7 %collective-permute-done.xa = f32[21,16,128]{2,1,0:T(8,128)S(1)} collective-permute-done((f32[21,16,128]{2,1,0:T(8,128)S(1)}, f32[21,16,128]{2,1,0:T(8,128)S(1)}, u32[]{:S(2)}, u32[]{:S(2)}) %collective-permute-start) | collective-permute-done | bytes 172064 | tf_op jit(solution)/shard_map/ppermute | solution.py:624
  8.6 0.0 collective-permute-done.1.xb
  8.6 0.1 collective-permute-start.4
  8.7 2.7 %collective-permute-start.5 = (f32[50,8,128]{2,1,0:T(8,128)S(1)}, f32[50,8,128]{2,1,0:T(8,128)S(1)}, u32[]{:S(2)}, u32[]{:S(2)}) collective-permute-start(f32[50,8,128]{2,1,0:T(8,128)S(1)} %get-tuple-element.34), channel_id=1, source_target_pairs={{0,7},{1,2},{2,1},{3,4},{4,3},{5,6},{6,5},{7,0},{8,15},{9,10},{10,... | collective-permute-start | bytes 614408 | tf_op jit(solution)/shard_map/ppermute | solution.py:624
  11.4 0.0 collective-permute-start.2
  11.4 0.6 %collective-permute-start.3 = (f32[48,8,128]{2,1,0:T(8,128)S(1)}, f32[48,8,128]{2,1,0:T(8,128)S(1)}, u32[]{:S(2)}, u32[]{:S(2)}) collective-permute-start(f32[48,8,128]{2,1,0:T(8,128)S(1)} %get-tuple-element.32), channel_id=1, source_target_pairs={{0,7},{1,2},{2,1},{3,4},{4,3},{5,6},{6,5},{7,0},{8,15},{9,10},{10,... | collective-permute-start | bytes 589832 | tf_op jit(solution)/shard_map/ppermute | solution.py:624
  12.1 14.8 %all_to_all.16 = f32[32,4,128]{2,1,0:T(4,128)S(1)} all-to-all(f32[32,4,128]{2,1,0:T(4,128)S(1)} %bitcast.6), channel_id=1, replica_groups=mesh['stream'=4,'trans'=8] {'stream','trans'}, dimensions={0} | all-to-all | bytes 131072 | tf_op jit(solution)/shard_map/all_to_all | solution.py:628
  26.9 3.2 %source.1 = f32[36,40,128]{2,1,0:T(8,128)S(1)} custom-call(f32[128,128]{1,0:T(8,128)S(1)} %bitcast.5), custom_call_target="tpu_custom_call" | custom-call | tf_op jit(solution)/shard_map/source/pallas_call | solution.py:682
  30.0 0.0 collective-permute-done.2.ya
  30.0 0.0 collective-permute-done.3.yb
  30.0 0.0 collective-permute-done.4.ca
  30.0 0.0 collective-permute-done.5.cb
  30.1 5.7 %presmooth.1 = (f32[32,8,128]{2,1,0:T(8,128)S(1)}, f32[40,48,128]{2,1,0:T(8,128)S(1)}, f32[40,48,128]{2,1,0:T(8,128)S(1)}, f32[40,48,128]{2,1,0:T(8,128)S(1)}, f...) custom-call(f32[16,16,128]{2,1,0:T(8,128)S(1)} %get-tuple-element.27, ...), custom_call_target="tpu_custom_call" | custom-call | tf_op jit(solution)/shard_map/presmooth/pallas_call | solution.py:695
  35.8 11.7 %all_to_all.17.slots = f32[32,8,128]{2,1,0:T(8,128)S(1)} all-to-all(f32[32,8,128]{2,1,0:T(8,128)S(1)} %get-tuple-element.36), channel_id=1, replica_groups=mesh['stream'=4,'trans'=8] {'stream','trans'}, dimensions={0} | all-to-all | bytes 262144 | tf_op jit(solution)/shard_map/all_to_all | solution.py:628
  47.5 4.4 %postsmooth.1 = f32[16,16,128]{2,1,0:T(8,128)} custom-call(f32[32,8,128]{2,1,0:T(8,128)S(1)} %all_to_all.17.slots, f32[40,48,128]{2,1,0:T(8,128)S(1)} %get-tuple-element.37.v0, f32[40,48,128]{2,1,0:T(8,128)S(1)} %get-tuple-element.38.b0, f32[40,48,128]{2,1,0:T(8,128)S(1)} %get-tuple-element.39.w0, f32[40,48,128]{2,1,0:T(8,128)S(1)} %get-tuple-element.40.cx0, ...), custom_call_target="tpu_custom_call" | custom-call | tf_op jit(solution)/shard_map/postsmooth/pallas_call | solution.py:717
  (1 shorter events, 0.0 us)
Async XLA Ops:
  1.1 7.5 %collective-permute-start = (f32[21,16,128]{2,1,0:T(8,128)S(1)}, f32[21,16,128]{2,1,0:T(8,128)S(1)}, u32[]{:S(2)}, u32[]{:S(2)}) collective-permute-start(f32[21,16,128]{2,1,0:T(8,128)S(1)} %get-tuple-element.29), channel_id=1, source_target_pairs={{0,8},{8,0},{16,24},{24,16},{1,9},{9,1},{17,25},{25,17},{2,10},{10... | collective-permute-start | bytes 516104 | tf_op jit(solution)/shard_map/ppermute | solution.py:624
  4.2 4.4 %collective-permute-start.1 = (f32[21,16,128]{2,1,0:T(8,128)S(1)}, f32[21,16,128]{2,1,0:T(8,128)S(1)}, u32[]{:S(2)}, u32[]{:S(2)}) collective-permute-start(f32[21,16,128]{2,1,0:T(8,128)S(1)} %get-tuple-element.30), channel_id=1, source_target_pairs={{8,16},{16,8},{9,17},{17,9},{10,18},{18,10},{11,19},{19,11},{12,20... | collective-permute-start | bytes 516104 | tf_op jit(solution)/shard_map/ppermute | solution.py:624
  8.6 21.4 %collective-permute-start.4 = (f32[50,8,128]{2,1,0:T(8,128)S(1)}, f32[50,8,128]{2,1,0:T(8,128)S(1)}, u32[]{:S(2)}, u32[]{:S(2)}) collective-permute-start(f32[50,8,128]{2,1,0:T(8,128)S(1)} %get-tuple-element.33), channel_id=1, source_target_pairs={{0,1},{1,0},{2,3},{3,2},{4,5},{5,4},{6,7},{7,6},{8,9},{9,8},{10,11... | collective-permute-start | bytes 614408 | tf_op jit(solution)/shard_map/ppermute | solution.py:624
  8.7 21.3 %collective-permute-start.5 = (f32[50,8,128]{2,1,0:T(8,128)S(1)}, f32[50,8,128]{2,1,0:T(8,128)S(1)}, u32[]{:S(2)}, u32[]{:S(2)}) collective-permute-start(f32[50,8,128]{2,1,0:T(8,128)S(1)} %get-tuple-element.34), channel_id=1, source_target_pairs={{0,7},{1,2},{2,1},{3,4},{4,3},{5,6},{6,5},{7,0},{8,15},{9,10},{10,... | collective-permute-start | bytes 614408 | tf_op jit(solution)/shard_map/ppermute | solution.py:624
  11.4 18.6 %collective-permute-start.2 = (f32[48,8,128]{2,1,0:T(8,128)S(1)}, f32[48,8,128]{2,1,0:T(8,128)S(1)}, u32[]{:S(2)}, u32[]{:S(2)}) collective-permute-start(f32[48,8,128]{2,1,0:T(8,128)S(1)} %get-tuple-element.31), channel_id=1, source_target_pairs={{0,1},{1,0},{2,3},{3,2},{4,5},{5,4},{6,7},{7,6},{8,9},{9,8},{10,11... | collective-permute-start | bytes 589832 | tf_op jit(solution)/shard_map/ppermute | solution.py:624
  11.4 18.6 %collective-permute-start.3 = (f32[48,8,128]{2,1,0:T(8,128)S(1)}, f32[48,8,128]{2,1,0:T(8,128)S(1)}, u32[]{:S(2)}, u32[]{:S(2)}) collective-permute-start(f32[48,8,128]{2,1,0:T(8,128)S(1)} %get-tuple-element.32), channel_id=1, source_target_pairs={{0,7},{1,2},{2,1},{3,4},{4,3},{5,6},{6,5},{7,0},{8,15},{9,10},{10,... | collective-permute-start | bytes 589832 | tf_op jit(solution)/shard_map/ppermute | solution.py:624

commit v3 on v2

--- a/solution.py
+++ b/solution.py
@@ -25,7 +25,7 @@
 FAR = 4
 R0 = 4
 ROWS0 = 48
-R1 = 8
+R1 = 12
 ROWS1 = 40
 SHIFT1 = 10
 
@@ -56,48 +56,76 @@
 
 
 def over(lo, hi, fn, limit=64, step=4):
+    def group(indices):
+        stores = [store for i in indices for store in fn(i) or ()]
+        for ref, index, value in stores:
+            ref[index] = value
+
     if hi - lo <= limit:
-        for i in range(lo, hi):
-            fn(i)
+        for i in range(lo, hi, step):
+            group(range(i, min(i + step, hi)))
         return
     whole = (hi - lo) // step
 
     def chunk(k, carry):
-        for j in range(step):
-            fn(lo + k * step + j)
+        group([lo + k * step + j for j in range(step)])
         return carry
 
     lax.fori_loop(0, whole, chunk, 0)
-    for i in range(lo + whole * step, hi):
-        fn(i)
-
-
-def quotient(scale, den):
-    return jnp.where(den > 0.0, scale / den, 0.0)
-
-
-def setup(rho, faces, w, dg, x0, x1, r0, nr, st, level):
+    group(range(lo + whole * step, hi))
+
+
+LEAST = 0.8 * air_density
+
+
+MEAN = 0.125
+DOWN = 4 * MEAN
+
+
+def face(den):
+    return 1.0 / jnp.maximum(den, LEAST)
+
+
+def pair(a, b):
+    a, b = jnp.maximum(a, LEAST), jnp.maximum(b, LEAST)
+    both = 1.0 / (a * b)
+    return both * b, both * a
+
+
+def setup(rho, faces, w, dg, x0, x1, r0, nr, st):
     cx, cy, cp = faces
-    scale = 2.0 * 0.25**level
     nz = rho.shape[-1]
     rows = pl.ds(r0, nr)
     lane = lanes((nr, nz))
     first, last = lane < st, lane >= nz - st
-    cx[x0 - 1, rows, :] = quotient(scale, rho[x0 - 1, rows, :] + rho[x0, rows, :])
+    cx[x0 - 1, rows, :] = face(rho[x0 - 1, rows, :] + rho[x0, rows, :])
 
     def plane(i):
         here = rho[i, rows, :]
-        fx = quotient(scale, here + rho[i + 1, rows, :])
-        cx[i, rows, :] = fx
-        cy[i, rows, :] = quotient(scale, here + rho[i, pl.ds(r0 + 1, nr), :])
-        fp = quotient(scale, here + jnp.where(last, 0.0, up(here, st)))
-        fm = jnp.where(first, quotient(scale, here), down(fp, st))
-        cp[i, rows, :] = jnp.where(last, 0.0, fp)
-        diag = fx + cx[i - 1, rows, :] + cy[i, rows, :] + cy[i, pl.ds(r0 - 1, nr), :] + fp + fm
-        dg[i, rows, :] = diag
-        w[i, rows, :] = jnp.where(here > 0.0, omega_factor / diag, 0.0)
-
-    over(x0, x1, plane)
+        fx, fy = pair(here + rho[i + 1, rows, :], here + rho[i, pl.ds(r0 + 1, nr), :])
+        fp, alone = pair(here + jnp.where(last, 0.0, up(here, st)), here)
+        fm = jnp.where(first, alone, down(fp, st))
+        at = (i, rows)
+        before = face(rho[i, pl.ds(r0 - 1, 1), :] + rho[i, pl.ds(r0, 1), :])
+        return (
+            (cy, (i, pl.ds(r0 - 1, 1)), before),
+            (cx, at, fx),
+            (cy, at, fy),
+            (cp, at, jnp.where(last, 0.0, fp)),
+            (dg, at, (fx + fy) + (fp + fm)),
+        )
+
+    over(x0, x1, plane, step=SETUP_STEP)
+
+    def diagonal(i):
+        at = (i, rows)
+        diag = dg[at] + (cx[i - 1, rows, :] + cy[i, pl.ds(r0 - 1, nr), :])
+        return (dg, at, diag), (w, at, jnp.where(rho[at] > 0.0, omega_factor / diag, 0.0))
+
+    over(x0, x1, diagonal)
+
+
+SETUP_STEP = 4
 
 
 def beside(v, faces, i, r0, nr, st):
@@ -116,7 +144,7 @@
     rows = pl.ds(r0, nr)
 
     def plane(i):
-        v[i, rows, :] = w[i, rows, :] * b[i, rows, :]
+        return ((v, (i, rows), w[i, rows, :] * b[i, rows, :]),)
 
     over(x0, x1, plane)
 
@@ -129,7 +157,7 @@
 
 def sweep(v, out, b, w, faces, x0, x1, r0, nr, st):
     def plane(i):
-        out[i, pl.ds(r0, nr), :] = swept(v, b, w, faces, i, r0, nr, st)
+        return ((out, (i, pl.ds(r0, nr)), swept(v, b, w, faces, i, r0, nr, st)),)
 
     over(x0, x1, plane)
 
@@ -140,19 +168,22 @@
     return b[i, rows, :] + (total - dg[i, rows, :] * here)
 
 
-def coarsen(fine, out, tmp, pairs, nr, st, to):
-    def pair(a, c):
-        total = fine(a) + fine(a + 1)
+def coarsen(factor, fine, out, tmp, pairs, nr, st, to):
+    a0, c0, count = pairs
+    half = nr // 2
+
+    def planes(k):
+        return ((tmp, (c0 + k, pl.ds(0, nr)), fine(a0 + 2 * k) + fine(a0 + 2 * k + 1)),)
+
+    def means(k):
+        c = c0 + k
+        total = tmp[c, pl.ds(0, half, stride=2), :] + tmp[c, pl.ds(1, half, stride=2), :]
         even = (lanes(total.shape) // st) % 2 == 0
         total = total + jnp.where(even, up(total, st), down(total, st))
-        tmp[c, pl.ds(0, nr), :] = total
-        half = nr // 2
-        out[c, pl.ds(to, half), :] = 0.125 * (
-            tmp[c, pl.ds(0, half, stride=2), :] + tmp[c, pl.ds(1, half, stride=2), :]
-        )
-
-    a0, c0, count = pairs
-    over(0, count, lambda k: pair(a0 + 2 * k, c0 + k))
+        return ((out, (c, pl.ds(to, half)), factor * total),)
+
+    over(0, count, planes, step=2)
+    over(0, count, means)
 
 
 def doubled(ref, k, row, value):
@@ -236,19 +267,24 @@
     s, t = lax.axis_index("stream"), lax.axis_index("trans")
     per_slab = disc.shape[0] // slabs
     part = per_slab // groups // 2
-    wide = ny + 2 * HALO
-    depth = lanes((8, nz))[:1]
-    for where_, first_x, count, to in ((-1, nx - HB, HB, 0), (0, 0, nx, HB), (1, 0, HB, HB + nx)):
-        slab = s + where_
-
-        def fill(slab=slab, first_x=first_x, count=count, to=to):
+    frame = out.shape[1]
+    cols = part * groups * nz
+    side = (frame - ny) // 2
+    for offset in (-1, 0, 1):
+        planes = []
+        for x in range(nx) if offset == 0 else range(nx - HB, nx) if offset < 0 else range(HB):
+            gap = 0 if offset == 0 else nx - x if offset < 0 else x + 1
+            edge = side if gap <= FAR else NEAR
+            planes.append((x, x + HB + offset * nx, side - edge, ny + 2 * edge))
+        slab = s + offset
+
+        def fill(planes=planes, slab=slab):
             base = pl.multiple_of(slab * per_slab, 8)
-            cols = part * groups * nz
             zrow = subs((nz, nz))
-            mrow = subs((count * wide, nz))
+            yrow = subs((frame, nz))
             for g in range(groups):
                 for p in range(part):
-                    at = (g * part + p) * nz
+                    at = pl.ds((g * part + p) * nz, nz)
                     tile = disc[pl.ds(base + (g * 2 * part) // 8 * 8, 8), :]
                     r = (g * 2 * part) % 8 + p
                     key = tile[r : r + 1].astype(jnp.int32)
@@ -257,40 +293,49 @@
                     y = (key >> log2(nz)) & (ny - 1)
                     x = (key >> log2(nz * ny)) & (nx - 1)
                     o = key >> log2(nz * ny * nx)
-                    row = (o - t) * ny + y + HALO
-                    ok = (row >= 0) & (row < wide) & (x >= first_x) & (x < first_x + count)
-                    m = jnp.where(ok, (x - first_x) * wide + row, -1)
-                    hot[pl.ds(0, count * wide), pl.ds(at, nz)] = (
-                        jnp.where(mrow == m, 1.0, 0.0).astype(BF16)
-                    )
+                    row = (o - t) * ny + y + side
+                    in_row = jnp.where(yrow == row, 1.0, 0.0).astype(BF16)
+                    in_near = None
+                    if len({first for _, _, first, _ in planes}) > 1:
+                        span = yrow[: ny + 2 * NEAR] + (side - NEAR)
+                        in_near = jnp.where(span == row, 1.0, 0.0).astype(BF16)
+                    to = 0
+                    for plane, _, first, count in planes:
+                        chosen = jnp.where(x == plane, 1.0, 0.0)
+                        chosen = jnp.broadcast_to(chosen, (16, nz)).astype(BF16)
+                        for k in range(count // 16):
+                            of = in_row if first % 16 == 0 else in_near
+                            row_at = first + 16 * k if first % 16 == 0 else 16 * k
+                            piece = of[row_at : row_at + 16]
+                            hot[pl.ds(to, 16), at] = piece * chosen
+                            to += 16
                     hi = f.astype(BF16).astype(F32)
-                    mid = (f - hi).astype(BF16).astype(F32)
-                    low = f - hi - mid
                     here = zrow == z
-                    for q, piece in enumerate((hi, mid, low)):
-                        val[pl.ds(q * nz, nz), pl.ds(at, nz)] = (
-                            jnp.where(here, piece, 0.0).astype(BF16)
-                        )
+                    for q, part_of in enumerate((hi, f - hi)):
+                        val[pl.ds(q * nz, nz), at] = jnp.where(here, part_of, 0.0).astype(BF16)
+            total = sum(count for _, _, _, count in planes)
             got = lax.dot_general(
-                hot[pl.ds(0, count * wide), pl.ds(0, cols)],
+                hot[pl.ds(0, total), pl.ds(0, cols)],
                 val[:, pl.ds(0, cols)],
                 (((1,), (1,)), ((), ())),
                 preferred_element_type=F32,
             )
-            got = got[:, :nz] + got[:, nz : 2 * nz] + got[:, 2 * nz :]
-            for i in range(count):
-                out[to + i] = got[i * wide : (i + 1) * wide]
-
-        if where_ == 0:
+            got = got[:, :nz] + got[:, nz:]
+            at = 0
+            for _, to, first, count in planes:
+                out[to, pl.ds(first, count), :] = got[at : at + count]
+                at += count
+
+        if offset == 0:
             fill()
         else:
-            inside = slab >= 0 if where_ < 0 else slab < slabs
+            inside = slab >= 0 if offset < 0 else slab < slabs
             pl.when(inside)(fill)
 
             @pl.when(jnp.logical_not(inside))
-            def _(count=count, to=to):
-                for i in range(count):
-                    out[to + i] = jnp.zeros(out.shape[1:], F32)
+            def _(planes=planes):
+                for _, to, first, count in planes:
+                    out[to, pl.ds(first, count), :] = jnp.zeros((count, nz), F32)
 
 
 def pre_kernel(
@@ -351,7 +396,9 @@
     wide = ny + 2 * HALO
     for i in range(nx + 2 * HB):
         at = HALO - HB + i
-        b0[at, pl.ds(R0, wide), :] = b0[at, pl.ds(R0, wide), :] + source[i]
+        gap = max(HALO - at, at - HALO - nx + 1)
+        rows = pl.ds(0, ROWS0) if gap <= FAR else pl.ds(own - NEAR, ny + 2 * NEAR)
+        b0[at, rows, :] = 0.5 * (b0[at, rows, :] + source[i, rows, :])
 
     f0 = (cx0, cy0, cp0)
     lo, hi = HALO - HB, HALO + nx + HB
@@ -361,12 +408,14 @@
             ref[i, pl.ds(R0 - 1, 1), :] = zero_row
         for ref in (u0, v0):
             ref[i, pl.ds(R0 + wide, 1), :] = zero_row
-    setup(rho0, f0, w0, dg0, lo, hi, R0, wide, 1, 0)
+    setup(rho0, f0, w0, dg0, lo, hi, R0, wide, 1)
     start(u0, b0, w0, lo, hi, R0, wide)
-    sweep(u0, v0, b0, w0, f0, lo + 1, hi - 1, R0, wide, 1)
+    inner, outer = HALO - 2, HALO + nx + 2
+    for x0, x1, cut in ((lo + 1, inner, 4), (inner, outer, 0), (outer, hi - 1, 4)):
+        sweep(u0, v0, b0, w0, f0, x0, x1, R0 + cut, wide - 2 * cut, 1)
 
     half = nx // 2 + HALO
-    wide1 = 24
+    wide1 = 16
     zero1 = jnp.zeros((ROWS1, nz), F32)
     for i in range(half):
         for ref in (rho1, b1, u1, v1, cy1):
@@ -378,15 +427,18 @@
         return rho0[i, pl.ds(R0, wide), :]
 
     rows_to = SHIFT1
-    coarsen(rho_rows, rho1, tmp0, (2, 1, half - 2), wide, 1, rows_to)
-
-    def res_rows(i):
-        return residual(v0, b0, dg0, f0, i, R0, wide, 1)
-
-    coarsen(res_rows, b1, tmp0, (lo + 2, (lo + 2) // 2, (hi - lo - 4) // 2), wide, 1, rows_to)
+    coarsen(MEAN, rho_rows, rho1, tmp0, (2, 1, half - 2), wide, 1, rows_to)
+
+    for x0, x1, cut in ((lo + 2, HALO - 4, 8), (HALO - 4, HALO + nx + 4, 4), (HALO + nx + 4, hi - 2, 8)):
+
+        def res_rows(i, cut=cut):
+            return residual(v0, b0, dg0, f0, i, R0 + cut, wide - 2 * cut, 1)
+
+        pairs = (x0, x0 // 2, (x1 - x0) // 2)
+        coarsen(DOWN, res_rows, b1, tmp0, pairs, wide - 2 * cut, 1, rows_to + cut // 2)
     f1 = (cx1, cy1, cp1)
     lo1, hi1 = (lo + 2) // 2, (hi - 2) // 2
-    setup(rho1, f1, w1, dg1, lo1, hi1, R1, wide1, 2, 1)
+    setup(rho1, f1, w1, dg1, lo1, hi1, R1, wide1, 2)
     start(u1, b1, w1, lo1, hi1, R1, wide1)
     sweep(u1, v1, b1, w1, f1, lo1 + 1, hi1 - 1, R1, wide1, 2)
 
@@ -394,23 +446,23 @@
     ny1 = ny // 2
     first1 = HALO // 2
 
-    def packed(fine):
-        total = None
+    def packed(factor, fine):
+        value = None
         for k in range(nx // 4):
-            a = first1 + 2 * k
-            pairs = fine(a) + fine(a + 1)
-            even = (lanes(pairs.shape) // 2) % 2 == 0
-            pairs = pairs + jnp.where(even, up(pairs, 2), down(pairs, 2))
-            turn = lanes(pairs.shape) % 4 == k
-            total = jnp.where(turn, pairs, 0.0 if total is None else total)
-        tmp1[...] = total
-        return 0.125 * (tmp1[pl.ds(0, ny1 // 2, stride=2), :] + tmp1[pl.ds(1, ny1 // 2, stride=2), :])
+            tmp1[k] = fine(first1 + 2 * k) + fine(first1 + 2 * k + 1)
+        for k in range(nx // 4):
+            total = tmp1[k, pl.ds(0, ny1 // 2, stride=2), :] + tmp1[k, pl.ds(1, ny1 // 2, stride=2), :]
+            even = (lanes(total.shape) // 2) % 2 == 0
+            total = total + jnp.where(even, up(total, 2), down(total, 2))
+            turn = lanes(total.shape) % 4 == k
+            value = jnp.where(turn, total, 0.0 if value is None else value)
+        return factor * value
 
     rows2 = ny1 // 2
     slots[0, pl.ds(0, rows2), :] = packed(
-        lambda i: residual(v1, b1, dg1, f1, i, own1, ny1, 2)
+        DOWN, lambda i: residual(v1, b1, dg1, f1, i, own1, ny1, 2)
     )
-    slots[0, pl.ds(rows2, rows2), :] = packed(lambda i: rho1[i, pl.ds(own1, ny1), :])
+    slots[0, pl.ds(rows2, rows2), :] = packed(MEAN, lambda i: rho1[i, pl.ds(own1, ny1), :])
     slot = slots[0]
 
     def put(g):
@@ -424,7 +476,6 @@
         self.rho, self.cx, self.cy, self.cp, self.w, self.dg, self.b, self.va, self.vb = refs
         self.planes, self.rows = planes, rows
         self.pitch, self.mult, self.st = 1 << k, mult >> k, mult << k
-        self.level = 2 + k
         lane = lanes((rows, nz))
         self.sub = (lane // self.pitch) % self.mult
         self.even_z = (lane // self.st) % 2 == 0
@@ -432,7 +483,7 @@
         self.at = pl.ds(8, rows)
 
     def each(self, fn):
-        over(1, 1 + self.planes, fn, 8, 2)
+        over(1, 1 + self.planes, fn, 8, 4)
 
     def next_x(self, here, above):
         if self.mult == 1:
@@ -447,26 +498,32 @@
         return jnp.where(self.sub == 0, far, down(here, self.pitch))
 
     def setup(self):
-        scale = 2.0 * 0.25**self.level
         rho, cx, cy, cp, at, n = self.rho, self.cx, self.cy, self.cp, self.at, self.rows
-        cx[0, at, :] = quotient(scale, self.next_x(rho[0, at, :], rho[1, at, :]))
+        cx[0, at, :] = face(self.next_x(rho[0, at, :], rho[1, at, :]))
 
         def plane(i):
             here = rho[i, at, :]
-            fx = quotient(scale, here + self.next_x(here, rho[i + 1, at, :]))
-            cx[i, at, :] = fx
-            cy[i, pl.ds(0, n + 8), :] = quotient(
-                scale, rho[i, pl.ds(0, n + 8), :] + rho[i, pl.ds(1, n + 8), :]
+            fx, fy = pair(
+                here + self.next_x(here, rho[i + 1, at, :]), here + rho[i, pl.ds(9, n), :]
             )
-            fp = quotient(scale, here + jnp.where(self.last, 0.0, up(here, self.st)))
-            fm = jnp.where(self.first, quotient(scale, here), down(fp, self.st))
-            cp[i, at, :] = jnp.where(self.last, 0.0, fp)
-            diag = fx + self.prev_x(fx, cx[i - 1, at, :]) + fp + fm
-            diag = diag + cy[i, at, :] + cy[i, pl.ds(7, n), :]
-            self.dg[i, at, :] = diag
-            self.w[i, at, :] = omega_factor / diag
+            fp, alone = pair(here + jnp.where(self.last, 0.0, up(here, self.st)), here)
+            fm = jnp.where(self.first, alone, down(fp, self.st))
+            return (
+                (cx, (i, at), fx),
+                (cy, (i, at), fy),
+                (cy, (i, pl.ds(7, 1)), face(rho[i, pl.ds(8, 1), :])),
+                (cp, (i, at), jnp.where(self.last, 0.0, fp)),
+                (self.dg, (i, at), (fx + fy) + (fp + fm)),
+            )
 
         self.each(plane)
+
+        def diagonal(i):
+            diag = self.prev_x(cx[i, at, :], cx[i - 1, at, :]) + cy[i, pl.ds(7, n), :]
+            diag = self.dg[i, at, :] + diag
+            return (self.dg, (i, at), diag), (self.w, (i, at), omega_factor / diag)
+
+        self.each(diagonal)
 
     def beside(self, v, i):
         at, n = self.at, self.rows
@@ -480,7 +537,7 @@
 
     def start(self):
         def plane(i):
-            self.va[i, self.at, :] = self.w[i, self.at, :] * self.b[i, self.at, :]
+            return ((self.va, (i, self.at), self.w[i, self.at, :] * self.b[i, self.at, :]),)
 
         self.each(plane)
 
@@ -489,9 +546,8 @@
 
             def plane(i):
                 here, total = self.beside(self.va, i)
-                self.vb[i, self.at, :] = (1.0 - omega_factor) * here + self.w[i, self.at, :] * (
-                    self.b[i, self.at, :] + total
-                )
+                new = self.w[i, self.at, :] * (self.b[i, self.at, :] + total)
+                return ((self.vb, (i, self.at), (1.0 - omega_factor) * here + new),)
 
             self.each(plane)
             self.va, self.vb = self.vb, self.va
@@ -500,26 +556,30 @@
         here, total = self.beside(self.va, i)
         return self.b[i, self.at, :] + (total - self.dg[i, self.at, :] * here)
 
-    def coarsen(self, fine, out, tmp):
-        def plane(i):
-            total = fine(i)
-            even_x = self.sub % 2 == 0
+    def coarsen(self, factor, fine, out, tmp):
+        half = self.rows // 2
+
+        def means(i):
+            total = tmp[i, pl.ds(0, half, stride=2), :] + tmp[i, pl.ds(1, half, stride=2), :]
+            even_x, even_z = self.sub[:half] % 2 == 0, self.even_z[:half]
             total = total + jnp.where(even_x, up(total, self.pitch), down(total, self.pitch))
-            total = total + jnp.where(self.even_z, up(total, self.st), down(total, self.st))
-            tmp[i, pl.ds(0, self.rows), :] = total
-            half = self.rows // 2
-            out[i, pl.ds(8, half), :] = 0.125 * (
-                tmp[i, pl.ds(0, half, stride=2), :] + tmp[i, pl.ds(1, half, stride=2), :]
+            total = total + jnp.where(even_z, up(total, self.st), down(total, self.st))
+            return ((out, (i, pl.ds(8, half)), factor * total),)
+
+        self.each(lambda i: ((tmp, (i, pl.ds(0, self.rows)), fine(i)),))
+        self.each(means)
+
+    def correct(self, below, tmp):
+        self.each(lambda i: doubled(tmp, i, 0, below.va[i, below.at, :]))
+        self.each(
+            lambda i: (
+                (
+                    self.va,
+                    (i, self.at),
+                    self.va[i, self.at, :] + tmp[i, pl.ds(0, self.rows), :],
+                ),
             )
-
-        self.each(plane)
-
-    def correct(self, below, tmp):
-        def plane(i):
-            doubled(tmp, i, 0, below.va[i, below.at, :])
-            self.va[i, self.at, :] = self.va[i, self.at, :] + tmp[i, pl.ds(0, self.rows), :]
-
-        self.each(plane)
+        )
 
 
 def post_kernel(slots, v0, b0, w0, cx0, cy0, cp0, v1, b1, w1, cx1, cy1, cp1, out, *refs):
@@ -553,16 +613,16 @@
 
     over(0, slabs, unpack, 8, 2)
     two.setup()
-    two.coarsen(lambda i: two.rho[i, two.at, :], three.rho, tmp)
+    two.coarsen(MEAN, lambda i: two.rho[i, two.at, :], three.rho, tmp)
     three.setup()
-    three.coarsen(lambda i: three.rho[i, three.at, :], four.rho, tmp)
+    three.coarsen(MEAN, lambda i: three.rho[i, three.at, :], four.rho, tmp)
     four.setup()
     two.start()
     two.smooth(1)
-    two.coarsen(two.residual, three.b, tmp)
+    two.coarsen(DOWN, two.residual, three.b, tmp)
     three.start()
     three.smooth(1)
-    three.coarsen(three.residual, four.b, tmp)
+    three.coarsen(DOWN, three.residual, four.b, tmp)
     four.start()
     four.smooth(CSWEEPS - 1)
     three.correct(four, tmp)
@@ -572,7 +632,7 @@
 
     f1 = (cx1, cy1, cp1)
     first1, nx1 = HALO // 2, nx // 2
-    wide1 = 24
+    wide1 = 16
     for i in range(e1.shape[0]):
         e1[i] = jnp.zeros((ROWS1, nz), F32)
     zero_row = jnp.zeros((1, nz), F32)
@@ -596,14 +656,14 @@
 
     f0 = (cx0, cy0, cp0)
     own = R0 + HALO
-    low, count = own - 8, ny + 16
+    low, count = own - 4, ny + 8
     for k in range(nx1 + 2):
         value = u1[first1 - 1 + k, pl.ds(SHIFT1 + first1 - 4, ny // 2 + 8), :]
-        doubled(e0, k, low, value)
+        doubled(e0, k, own - 8, value)
     for i in range(HALO - 2, HALO + nx + 2):
         rows0 = pl.ds(low, count)
         u0[i, rows0, :] = v0[i, rows0, :] + e0[(i - HALO + 2) // 2, rows0, :]
-    sweep(u0, x0, b0, w0, f0, HALO - 1, HALO + nx + 1, low + 7, count - 8, 1)
+    sweep(u0, x0, b0, w0, f0, HALO - 1, HALO + nx + 1, low, count, 1)
     for i in range(nx):
         out[i] = swept(x0, b0, w0, f0, HALO + i, own, ny, 1)
 
@@ -637,7 +697,6 @@
     slabs, groups = lax.axis_size("stream"), lax.axis_size("trans")
     devices = slabs * groups
     rows = disc_cell.shape[1] // nz
-    wide = ny + 2 * HALO
     halo_x = sds(HB + HD, ny, nz)
     halo_y = sds(3 * nx, 8, nz)
     corner = sds(2 * (HB + HD + FAR), 8, nz)
@@ -681,10 +740,10 @@
     cols = groups * rows * nz
     source = pl.pallas_call(
         functools.partial(source_kernel, (nx, ny, nz)),
-        out_shape=sds(nx + 2 * HB, wide, nz),
+        out_shape=sds(nx + 2 * HB, ROWS0, nz),
         scratch_shapes=[
-            pltpu.VMEM((nx * wide, cols), BF16),
-            pltpu.VMEM((3 * nz, cols), BF16),
+            pltpu.VMEM((nx * ROWS0, cols), BF16),
+            pltpu.VMEM((2 * nz, cols), BF16),
         ],
         compiler_params=params(24),
         name="source",
@@ -697,7 +756,7 @@
         out_shape=(sds(devices, 8, nz), *([frame0] * 6), *([frame1] * 6)),
         scratch_shapes=[
             s0, s0, s0, s1, s1, s1,
-            pltpu.VMEM((half, ROWS0, nz), F32), pltpu.VMEM((ny // 2, nz), F32),
+            pltpu.VMEM((half, ROWS0, nz), F32), pltpu.VMEM((nx // 4, ny // 2, nz), F32),
         ],
         compiler_params=params(28),
         name="presmooth",
@@ -718,7 +777,7 @@
         post_kernel,
         out_shape=sds(nx, ny, nz),
         scratch_shapes=scratch,
-        compiler_params=params(28),
+        compiler_params=params(32),
         name="postsmooth",
     )(slots, *state)
 

time: 52.1 us -> 48.6 us (0.933)
  Pallas kernels: 14.4 us -> 11.3 us
    pallas_call x1, Pallas kernels: 5.72 us -> 4.18 us  [body(): pl.pallas_call(pre_kernel, out_shape=(sds(devices, 8, nz), *[frame0] * 6,...]
    pallas_call x1, Pallas kernels: 3.15 us -> 2.33 us  [body(): pl.pallas_call(functools.partial(source_kernel, (nx, ny, nz)), out_shape=...]
    pallas_call x1, Pallas kernels: 4.38 us -> 3.63 us  [body(): pl.pallas_call(post_kernel, out_shape=sds(nx, ny, nz), scratch_shapes=scr...]
  transfers between devices with their start and end apart: 6 -> 6, of which waited for: 1 -> 1; matrix products, arithmetic and copies ran while one was open for 0% -> 0% of each run, Pallas kernels for 6% -> 5%
where the time goes in v3:
time: 48.6 us; the launch traced here: 48.4 us
  blocking collectives  26.1 us (54%)
  Pallas kernels  11.3 us (23%)
  starting transfers between devices  7.21 us (15%)
  waiting for transfers between devices  3.72 us (8%)
    all_to_all x2, blocking collectives, gather(): return lax.all_to_all(value, AXES, 0, 0, tiled=True)  26.1 us
    ppermute x6, starting transfers between devices, swap(): return lax.ppermute(value, axis, exchange(count, parity, open_ends))  7.21 us
    pallas_call x1, Pallas kernels, body(): pl.pallas_call(pre_kernel, out_shape=(sds(devices, 8, nz), *[frame0] * 6,...  4.18 us
    ppermute x6, waiting for transfers between devices, swap(): return lax.ppermute(value, axis, exchange(count, parity, open_ends))  3.72 us
    pallas_call x1, Pallas kernels, body(): pl.pallas_call(post_kernel, out_shape=sds(nx, ny, nz), scratch_shapes=scr...  3.63 us
    pallas_call x1, Pallas kernels, body(): pl.pallas_call(functools.partial(source_kernel, (nx, ny, nz)), out_shape=...  2.33 us
    pallas_call x1, Pallas kernels, body(): pl.pallas_call(functools.partial(pack_kernel, devices), out_shape=(block,...  1.09 us
  transfers between devices with their start and end apart: 6, of which 1 were waited for; matrix products, arithmetic and copies ran while one was open for 0% of the time, Pallas kernels for 5%

profile of v3, /device:TPU:0, one launch (start us, length us, event | category | flops | bytes accessed | tf_op | source)
XLA Modules:
  0.0 48.4 jit_solution(14975474997990861135)
XLA Ops:
  0.0 1.1 %pack.1 = (f32[16,16,128]{2,1,0:T(8,128)S(1)}, f32[16,16,128]{2,1,0:T(8,128)S(1)}, f32[21,16,128]{2,1,0:T(8,128)S(1)}, f32[21,16,128]{2,1,0:T(8,128)S(1)}, f32[4...) custom-call(f32[16,16,128]{2,1,0:T(8,128)} %refs_0_.1, s32[16,16,128]{2,1,0:T(8,128)} %refs_1_.1, ...), custom_call_target="tpu_custom_call" | custom-call | tf_op jit(solution)/shard_map/pack/pallas_call | solution.py:705
  1.1 3.1 %collective-permute-start = (f32[21,16,128]{2,1,0:T(8,128)S(1)}, f32[21,16,128]{2,1,0:T(8,128)S(1)}, u32[]{:S(2)}, u32[]{:S(2)}) collective-permute-start(f32[21,16,128]{2,1,0:T(8,128)S(1)} %get-tuple-element.29), channel_id=1, source_target_pairs={{0,8},{8,0},{16,24},{24,16},{1,9},{9,1},{17,25},{25,17},{2,10},{10... | collective-permute-start | bytes 516104 | tf_op jit(solution)/shard_map/ppermute | solution.py:684
  4.2 0.7 %collective-permute-start.1 = (f32[21,16,128]{2,1,0:T(8,128)S(1)}, f32[21,16,128]{2,1,0:T(8,128)S(1)}, u32[]{:S(2)}, u32[]{:S(2)}) collective-permute-start(f32[21,16,128]{2,1,0:T(8,128)S(1)} %get-tuple-element.30), channel_id=1, source_target_pairs={{8,16},{16,8},{9,17},{17,9},{10,18},{18,10},{11,19},{19,11},{12,20... | collective-permute-start | bytes 516104 | tf_op jit(solution)/shard_map/ppermute | solution.py:684
  4.9 3.7 %collective-permute-done.xa = f32[21,16,128]{2,1,0:T(8,128)S(1)} collective-permute-done((f32[21,16,128]{2,1,0:T(8,128)S(1)}, f32[21,16,128]{2,1,0:T(8,128)S(1)}, u32[]{:S(2)}, u32[]{:S(2)}) %collective-permute-start) | collective-permute-done | bytes 172064 | tf_op jit(solution)/shard_map/ppermute | solution.py:684
  8.6 0.0 collective-permute-done.1.xb
  8.6 0.1 collective-permute-start.4
  8.7 2.7 %collective-permute-start.5 = (f32[50,8,128]{2,1,0:T(8,128)S(1)}, f32[50,8,128]{2,1,0:T(8,128)S(1)}, u32[]{:S(2)}, u32[]{:S(2)}) collective-permute-start(f32[50,8,128]{2,1,0:T(8,128)S(1)} %get-tuple-element.34), channel_id=1, source_target_pairs={{0,7},{1,2},{2,1},{3,4},{4,3},{5,6},{6,5},{7,0},{8,15},{9,10},{10,... | collective-permute-start | bytes 614408 | tf_op jit(solution)/shard_map/ppermute | solution.py:684
  11.4 0.0 collective-permute-start.2
  11.4 0.6 %collective-permute-start.3 = (f32[48,8,128]{2,1,0:T(8,128)S(1)}, f32[48,8,128]{2,1,0:T(8,128)S(1)}, u32[]{:S(2)}, u32[]{:S(2)}) collective-permute-start(f32[48,8,128]{2,1,0:T(8,128)S(1)} %get-tuple-element.32), channel_id=1, source_target_pairs={{0,7},{1,2},{2,1},{3,4},{4,3},{5,6},{6,5},{7,0},{8,15},{9,10},{10,... | collective-permute-start | bytes 589832 | tf_op jit(solution)/shard_map/ppermute | solution.py:684
  12.1 14.8 %all_to_all.16 = f32[32,4,128]{2,1,0:T(4,128)S(1)} all-to-all(f32[32,4,128]{2,1,0:T(4,128)S(1)} %bitcast.6), channel_id=1, replica_groups=mesh['stream'=4,'trans'=8] {'stream','trans'}, dimensions={0} | all-to-all | bytes 131072 | tf_op jit(solution)/shard_map/all_to_all | solution.py:688
  26.9 2.3 %source.1 = f32[36,48,128]{2,1,0:T(8,128)S(1)} custom-call(f32[128,128]{1,0:T(8,128)S(1)} %bitcast.5), custom_call_target="tpu_custom_call" | custom-call | tf_op jit(solution)/shard_map/source/pallas_call | solution.py:741
  29.2 0.0 collective-permute-done.2.ya
  29.2 0.0 collective-permute-done.3.yb
  29.2 0.0 collective-permute-done.4.ca
  29.2 0.0 collective-permute-done.5.cb
  29.2 4.2 %presmooth.1 = (f32[32,8,128]{2,1,0:T(8,128)S(1)}, f32[40,48,128]{2,1,0:T(8,128)S(1)}, f32[40,48,128]{2,1,0:T(8,128)S(1)}, f32[40,48,128]{2,1,0:T(8,128)S(1)}, f...) custom-call(f32[16,16,128]{2,1,0:T(8,128)S(1)} %get-tuple-element.27, ...), custom_call_target="tpu_custom_call" | custom-call | tf_op jit(solution)/shard_map/presmooth/pallas_call | solution.py:754
  33.4 11.4 %all_to_all.17.slots = f32[32,8,128]{2,1,0:T(8,128)S(1)} all-to-all(f32[32,8,128]{2,1,0:T(8,128)S(1)} %get-tuple-element.36), channel_id=1, replica_groups=mesh['stream'=4,'trans'=8] {'stream','trans'}, dimensions={0} | all-to-all | bytes 262144 | tf_op jit(solution)/shard_map/all_to_all | solution.py:688
  44.8 3.6 %postsmooth.1 = f32[16,16,128]{2,1,0:T(8,128)} custom-call(f32[32,8,128]{2,1,0:T(8,128)S(1)} %all_to_all.17.slots, f32[40,48,128]{2,1,0:T(8,128)S(1)} %get-tuple-element.37.v0, f32[40,48,128]{2,1,0:T(8,128)S(1)} %get-tuple-element.38.b0, f32[40,48,128]{2,1,0:T(8,128)S(1)} %get-tuple-element.39.w0, f32[40,48,128]{2,1,0:T(8,128)S(1)} %get-tuple-element.40.cx0, ...), custom_call_target="tpu_custom_call" | custom-call | tf_op jit(solution)/shard_map/postsmooth/pallas_call | solution.py:776
  (1 shorter events, 0.0 us)
Async XLA Ops:
  1.1 7.5 %collective-permute-start = (f32[21,16,128]{2,1,0:T(8,128)S(1)}, f32[21,16,128]{2,1,0:T(8,128)S(1)}, u32[]{:S(2)}, u32[]{:S(2)}) collective-permute-start(f32[21,16,128]{2,1,0:T(8,128)S(1)} %get-tuple-element.29), channel_id=1, source_target_pairs={{0,8},{8,0},{16,24},{24,16},{1,9},{9,1},{17,25},{25,17},{2,10},{10... | collective-permute-start | bytes 516104 | tf_op jit(solution)/shard_map/ppermute | solution.py:684
  4.2 4.4 %collective-permute-start.1 = (f32[21,16,128]{2,1,0:T(8,128)S(1)}, f32[21,16,128]{2,1,0:T(8,128)S(1)}, u32[]{:S(2)}, u32[]{:S(2)}) collective-permute-start(f32[21,16,128]{2,1,0:T(8,128)S(1)} %get-tuple-element.30), channel_id=1, source_target_pairs={{8,16},{16,8},{9,17},{17,9},{10,18},{18,10},{11,19},{19,11},{12,20... | collective-permute-start | bytes 516104 | tf_op jit(solution)/shard_map/ppermute | solution.py:684
  8.6 20.6 %collective-permute-start.4 = (f32[50,8,128]{2,1,0:T(8,128)S(1)}, f32[50,8,128]{2,1,0:T(8,128)S(1)}, u32[]{:S(2)}, u32[]{:S(2)}) collective-permute-start(f32[50,8,128]{2,1,0:T(8,128)S(1)} %get-tuple-element.33), channel_id=1, source_target_pairs={{0,1},{1,0},{2,3},{3,2},{4,5},{5,4},{6,7},{7,6},{8,9},{9,8},{10,11... | collective-permute-start | bytes 614408 | tf_op jit(solution)/shard_map/ppermute | solution.py:684
  8.7 20.5 %collective-permute-start.5 = (f32[50,8,128]{2,1,0:T(8,128)S(1)}, f32[50,8,128]{2,1,0:T(8,128)S(1)}, u32[]{:S(2)}, u32[]{:S(2)}) collective-permute-start(f32[50,8,128]{2,1,0:T(8,128)S(1)} %get-tuple-element.34), channel_id=1, source_target_pairs={{0,7},{1,2},{2,1},{3,4},{4,3},{5,6},{6,5},{7,0},{8,15},{9,10},{10,... | collective-permute-start | bytes 614408 | tf_op jit(solution)/shard_map/ppermute | solution.py:684
  11.4 17.8 %collective-permute-start.2 = (f32[48,8,128]{2,1,0:T(8,128)S(1)}, f32[48,8,128]{2,1,0:T(8,128)S(1)}, u32[]{:S(2)}, u32[]{:S(2)}) collective-permute-start(f32[48,8,128]{2,1,0:T(8,128)S(1)} %get-tuple-element.31), channel_id=1, source_target_pairs={{0,1},{1,0},{2,3},{3,2},{4,5},{5,4},{6,7},{7,6},{8,9},{9,8},{10,11... | collective-permute-start | bytes 589832 | tf_op jit(solution)/shard_map/ppermute | solution.py:684
  11.4 17.8 %collective-permute-start.3 = (f32[48,8,128]{2,1,0:T(8,128)S(1)}, f32[48,8,128]{2,1,0:T(8,128)S(1)}, u32[]{:S(2)}, u32[]{:S(2)}) collective-permute-start(f32[48,8,128]{2,1,0:T(8,128)S(1)} %get-tuple-element.32), channel_id=1, source_target_pairs={{0,7},{1,2},{2,1},{3,4},{4,3},{5,6},{6,5},{7,0},{8,15},{9,10},{10,... | collective-permute-start | bytes 589832 | tf_op jit(solution)/shard_map/ppermute | solution.py:684

commit v4 on v3

--- a/solution.py
+++ b/solution.py
@@ -23,6 +23,8 @@
 HD = 11
 NEAR = 8
 FAR = 4
+THIN = 3
+CORNER = HB + HD - THIN + FAR
 R0 = 4
 ROWS0 = 48
 R1 = 12
@@ -246,19 +248,32 @@
     t_even = lax.axis_index("trans") % 2 == 0
     base = 0
     for x, high in ((xa, s_even), (xb, jnp.logical_not(s_even))):
-        for i in range(HB + HD):
+
+        def rows(i):
             tile = x[i]
             low_rows, high_rows = tile[:NEAR], tile[ny - NEAR :]
-            ca[base + i] = jnp.where(t_even, high_rows, low_rows)
-            cb[base + i] = jnp.where(t_even, low_rows, high_rows)
+            return jnp.where(t_even, high_rows, low_rows), jnp.where(t_even, low_rows, high_rows)
+
+        at = base
+        for first, count in ((0, HB), (HB, HD)):
+            of = first + jnp.where(high, 0, THIN)
+            for i in range(count - THIN):
+                ca[at], cb[at] = rows(of + i)
+                at += 1
+        for i in range(THIN):
+            b = rows(jnp.where(high, HB - THIN + i, THIN - 1 - i))
+            d = rows(HB + jnp.where(high, HD - THIN + i, THIN - 1 - i))
+            ca[at] = half_tile(b[0], d[0], t_even)
+            cb[at] = half_tile(b[1], d[1], jnp.logical_not(t_even))
+            at += 1
         at_b = jnp.where(high, 0, HB - FAR)
         at_d = jnp.where(high, HB, HB + HD - FAR)
         for i in range(FAR):
             mid_b = x[at_b + i, pl.ds(FAR, 8), :]
             mid_d = x[at_d + i, pl.ds(FAR, 8), :]
-            ca[base + HB + HD + i] = half_tile(mid_b, mid_d, jnp.logical_not(t_even))
-            cb[base + HB + HD + i] = half_tile(mid_b, mid_d, t_even)
-        base += HB + HD + FAR
+            ca[at + i] = half_tile(mid_b, mid_d, jnp.logical_not(t_even))
+            cb[at + i] = half_tile(mid_b, mid_d, t_even)
+        base += CORNER
 
 
 def source_kernel(shape, disc, out, hot, val):
@@ -294,21 +309,17 @@
                     x = (key >> log2(nz * ny)) & (nx - 1)
                     o = key >> log2(nz * ny * nx)
                     row = (o - t) * ny + y + side
-                    in_row = jnp.where(yrow == row, 1.0, 0.0).astype(BF16)
-                    in_near = None
-                    if len({first for _, _, first, _ in planes}) > 1:
-                        span = yrow[: ny + 2 * NEAR] + (side - NEAR)
-                        in_near = jnp.where(span == row, 1.0, 0.0).astype(BF16)
+                    in_row = jnp.where(yrow == row, 1.0, 0.0)
+                    place = jnp.broadcast_to(x, (8, nz))
                     to = 0
                     for plane, _, first, count in planes:
-                        chosen = jnp.where(x == plane, 1.0, 0.0)
-                        chosen = jnp.broadcast_to(chosen, (16, nz)).astype(BF16)
-                        for k in range(count // 16):
-                            of = in_row if first % 16 == 0 else in_near
-                            row_at = first + 16 * k if first % 16 == 0 else 16 * k
-                            piece = of[row_at : row_at + 16]
-                            hot[pl.ds(to, 16), at] = piece * chosen
-                            to += 16
+                        here = place == plane
+                        parts = [
+                            jnp.where(here, in_row[first + k : first + k + 8], 0.0)
+                            for k in range(0, count, 8)
+                        ]
+                        hot[pl.ds(to, count), at] = jnp.concatenate(parts, 0).astype(BF16)
+                        to += count
                     hi = f.astype(BF16).astype(F32)
                     here = zrow == z
                     for q, part_of in enumerate((hi, f - hi)):
@@ -380,19 +391,26 @@
         far(HALO + i, ya[2 * nx + i], yb[2 * nx + i])
     base = 0
     for x, high in ((xa, s_even), (xb, jnp.logical_not(s_even))):
-        at_b = jnp.where(high, HALO + nx, HALO - HB)
-        at_d = jnp.where(high, HALO + nx, HALO - HD)
-        at_f = jnp.where(high, HALO + nx, HALO - FAR)
-        for i in range(HB):
-            b0[at_b + i, pl.ds(own, ny), :] = x[i]
-            near(b0, at_b + i, ca[base + i], cb[base + i])
-        for i in range(HD):
-            rho0[at_d + i, pl.ds(own, ny), :] = x[HB + i]
-            near(rho0, at_d + i, ca[base + HB + i], cb[base + HB + i])
+        at = base
+        for ref, first, count in ((b0, 0, HB), (rho0, HB, HD)):
+            to = jnp.where(high, HALO + nx, HALO - count)
+            for i in range(count):
+                ref[to + i, pl.ds(own, ny), :] = x[first + i]
+            to = jnp.where(high, HALO + nx, HALO - count + THIN)
+            for i in range(count - THIN):
+                near(ref, to + i, ca[at], cb[at])
+                at += 1
+        for i in range(THIN):
+            low, top = sides(ca[at], cb[at])
+            at += 1
+            for ref, count, part in ((b0, HB, 0), (rho0, HD, FAR)):
+                to = jnp.where(high, HALO + nx + count - THIN + i, HALO - count + THIN - 1 - i)
+                ref[to, pl.ds(own - FAR, FAR), :] = low[part : part + FAR]
+                ref[to, pl.ds(own + ny, FAR), :] = top[part : part + FAR]
+        to = jnp.where(high, HALO + nx, HALO - FAR)
         for i in range(FAR):
-            k = base + HB + HD + i
-            far(at_f + i, ca[k], cb[k])
-        base += HB + HD + FAR
+            far(to + i, ca[at + i], cb[at + i])
+        base += CORNER
     wide = ny + 2 * HALO
     for i in range(nx + 2 * HB):
         at = HALO - HB + i
@@ -699,7 +717,7 @@
     rows = disc_cell.shape[1] // nz
     halo_x = sds(HB + HD, ny, nz)
     halo_y = sds(3 * nx, 8, nz)
-    corner = sds(2 * (HB + HD + FAR), 8, nz)
+    corner = sds(2 * CORNER, 8, nz)
 
     block, row = sds(nx, ny, nz), pltpu.VMEM((rows, nz), jnp.int32)
     rhs, dens, xa, xb, ya, yb, disc = pl.pallas_call(

time: 48.6 us -> 45.2 us (0.930)
  waiting for transfers between devices: 3.72 us -> 1.09 us
  blocking collectives: 26.1 us -> 23.5 us
  starting transfers between devices: 7.21 us -> 9.18 us
    all_to_all x2, blocking collectives: 26.1 us -> 23.5 us  [gather(): return lax.all_to_all(value, AXES, 0, 0, tiled=True)]
    ppermute x6, waiting for transfers between devices: 3.72 us -> 1.09 us  [swap(): return lax.ppermute(value, axis, exchange(count, parity, open_ends))]
    ppermute x6, starting transfers between devices: 7.21 us -> 9.18 us  [swap(): return lax.ppermute(value, axis, exchange(count, parity, open_ends))]
where the time goes in v4:
time: 45.2 us; the launch traced here: 45 us
  blocking collectives  23.5 us (52%)
  Pallas kernels  11.2 us (25%)
  starting transfers between devices  9.18 us (20%)
  waiting for transfers between devices  1.09 us (2%)
    all_to_all x2, blocking collectives, gather(): return lax.all_to_all(value, AXES, 0, 0, tiled=True)  23.5 us
    ppermute x6, starting transfers between devices, swap(): return lax.ppermute(value, axis, exchange(count, parity, open_ends))  9.18 us
    pallas_call x1, Pallas kernels, body(): pl.pallas_call(pre_kernel, out_shape=(sds(devices, 8, nz), *[frame0] * 6,...  4.09 us
    pallas_call x1, Pallas kernels, body(): pl.pallas_call(post_kernel, out_shape=sds(nx, ny, nz), scratch_shapes=scr...  3.6 us
    pallas_call x1, Pallas kernels, body(): pl.pallas_call(functools.partial(source_kernel, (nx, ny, nz)), out_shape=...  2.34 us
    ppermute x6, waiting for transfers between devices, swap(): return lax.ppermute(value, axis, exchange(count, parity, open_ends))  1.09 us
    pallas_call x1, Pallas kernels, body(): pl.pallas_call(functools.partial(pack_kernel, devices), out_shape=(block,...  1.09 us
  transfers between devices with their start and end apart: 6, of which 1 were waited for; matrix products, arithmetic and copies ran while one was open for 0% of the time, Pallas kernels for 5%

profile of v4, /device:TPU:0, one launch (start us, length us, event | category | flops | bytes accessed | tf_op | source)
XLA Modules:
  0.0 45.0 jit_solution(16780251122948790808)
XLA Ops:
  0.0 1.1 %pack.1 = (f32[16,16,128]{2,1,0:T(8,128)S(1)}, f32[16,16,128]{2,1,0:T(8,128)S(1)}, f32[21,16,128]{2,1,0:T(8,128)S(1)}, f32[21,16,128]{2,1,0:T(8,128)S(1)}, f32[4...) custom-call(f32[16,16,128]{2,1,0:T(8,128)} %refs_0_.1, s32[16,16,128]{2,1,0:T(8,128)} %refs_1_.1, ...), custom_call_target="tpu_custom_call" | custom-call | tf_op jit(solution)/shard_map/pack/pallas_call | solution.py:723
  1.1 3.1 %collective-permute-start = (f32[21,16,128]{2,1,0:T(8,128)S(1)}, f32[21,16,128]{2,1,0:T(8,128)S(1)}, u32[]{:S(2)}, u32[]{:S(2)}) collective-permute-start(f32[21,16,128]{2,1,0:T(8,128)S(1)} %get-tuple-element.29), channel_id=1, source_target_pairs={{0,8},{8,0},{16,24},{24,16},{1,9},{9,1},{17,25},{25,17},{2,10},{10... | collective-permute-start | bytes 516104 | tf_op jit(solution)/shard_map/ppermute | solution.py:702
  4.2 0.7 %collective-permute-start.1 = (f32[21,16,128]{2,1,0:T(8,128)S(1)}, f32[21,16,128]{2,1,0:T(8,128)S(1)}, u32[]{:S(2)}, u32[]{:S(2)}) collective-permute-start(f32[21,16,128]{2,1,0:T(8,128)S(1)} %get-tuple-element.30), channel_id=1, source_target_pairs={{8,16},{16,8},{9,17},{17,9},{10,18},{18,10},{11,19},{19,11},{12,20... | collective-permute-start | bytes 516104 | tf_op jit(solution)/shard_map/ppermute | solution.py:702
  4.9 0.1 collective-permute-start.2
  5.0 2.5 %collective-permute-start.3 = (f32[48,8,128]{2,1,0:T(8,128)S(1)}, f32[48,8,128]{2,1,0:T(8,128)S(1)}, u32[]{:S(2)}, u32[]{:S(2)}) collective-permute-start(f32[48,8,128]{2,1,0:T(8,128)S(1)} %get-tuple-element.32), channel_id=1, source_target_pairs={{0,7},{1,2},{2,1},{3,4},{4,3},{5,6},{6,5},{7,0},{8,15},{9,10},{10,... | collective-permute-start | bytes 589832 | tf_op jit(solution)/shard_map/ppermute | solution.py:702
  7.5 1.1 %collective-permute-done.xa = f32[21,16,128]{2,1,0:T(8,128)S(1)} collective-permute-done((f32[21,16,128]{2,1,0:T(8,128)S(1)}, f32[21,16,128]{2,1,0:T(8,128)S(1)}, u32[]{:S(2)}, u32[]{:S(2)}) %collective-permute-start) | collective-permute-done | bytes 172064 | tf_op jit(solution)/shard_map/ppermute | solution.py:702
  8.6 0.0 collective-permute-done.1.xb
  8.6 0.1 collective-permute-start.4
  8.7 2.7 %collective-permute-start.5 = (f32[44,8,128]{2,1,0:T(8,128)S(1)}, f32[44,8,128]{2,1,0:T(8,128)S(1)}, u32[]{:S(2)}, u32[]{:S(2)}) collective-permute-start(f32[44,8,128]{2,1,0:T(8,128)S(1)} %get-tuple-element.34), channel_id=1, source_target_pairs={{0,7},{1,2},{2,1},{3,4},{4,3},{5,6},{6,5},{7,0},{8,15},{9,10},{10,... | collective-permute-start | bytes 540680 | tf_op jit(solution)/shard_map/ppermute | solution.py:702
  11.4 13.3 %all_to_all.16 = f32[32,4,128]{2,1,0:T(4,128)S(1)} all-to-all(f32[32,4,128]{2,1,0:T(4,128)S(1)} %bitcast.6), channel_id=1, replica_groups=mesh['stream'=4,'trans'=8] {'stream','trans'}, dimensions={0} | all-to-all | bytes 131072 | tf_op jit(solution)/shard_map/all_to_all | solution.py:706
  24.8 2.3 %source.1 = f32[36,48,128]{2,1,0:T(8,128)S(1)} custom-call(f32[128,128]{1,0:T(8,128)S(1)} %bitcast.5), custom_call_target="tpu_custom_call" | custom-call | tf_op jit(solution)/shard_map/source/pallas_call | solution.py:759
  27.1 0.0 collective-permute-done.2.ya
  27.1 0.0 collective-permute-done.3.yb
  27.1 0.0 collective-permute-done.4.ca
  27.1 0.0 collective-permute-done.5.cb
  27.2 4.1 %presmooth.1 = (f32[32,8,128]{2,1,0:T(8,128)S(1)}, f32[40,48,128]{2,1,0:T(8,128)S(1)}, f32[40,48,128]{2,1,0:T(8,128)S(1)}, f32[40,48,128]{2,1,0:T(8,128)S(1)}, f...) custom-call(f32[16,16,128]{2,1,0:T(8,128)S(1)} %get-tuple-element.27, ...), custom_call_target="tpu_custom_call" | custom-call | tf_op jit(solution)/shard_map/presmooth/pallas_call | solution.py:772
  31.3 10.2 %all_to_all.17.slots = f32[32,8,128]{2,1,0:T(8,128)S(1)} all-to-all(f32[32,8,128]{2,1,0:T(8,128)S(1)} %get-tuple-element.36), channel_id=1, replica_groups=mesh['stream'=4,'trans'=8] {'stream','trans'}, dimensions={0} | all-to-all | bytes 262144 | tf_op jit(solution)/shard_map/all_to_all | solution.py:706
  41.4 3.6 %postsmooth.1 = f32[16,16,128]{2,1,0:T(8,128)} custom-call(f32[32,8,128]{2,1,0:T(8,128)S(1)} %all_to_all.17.slots, f32[40,48,128]{2,1,0:T(8,128)S(1)} %get-tuple-element.37.v0, f32[40,48,128]{2,1,0:T(8,128)S(1)} %get-tuple-element.38.b0, f32[40,48,128]{2,1,0:T(8,128)S(1)} %get-tuple-element.39.w0, f32[40,48,128]{2,1,0:T(8,128)S(1)} %get-tuple-element.40.cx0, ...), custom_call_target="tpu_custom_call" | custom-call | tf_op jit(solution)/shard_map/postsmooth/pallas_call | solution.py:794
  (1 shorter events, 0.0 us)
Async XLA Ops:
  1.1 7.5 %collective-permute-start = (f32[21,16,128]{2,1,0:T(8,128)S(1)}, f32[21,16,128]{2,1,0:T(8,128)S(1)}, u32[]{:S(2)}, u32[]{:S(2)}) collective-permute-start(f32[21,16,128]{2,1,0:T(8,128)S(1)} %get-tuple-element.29), channel_id=1, source_target_pairs={{0,8},{8,0},{16,24},{24,16},{1,9},{9,1},{17,25},{25,17},{2,10},{10... | collective-permute-start | bytes 516104 | tf_op jit(solution)/shard_map/ppermute | solution.py:702
  4.2 4.4 %collective-permute-start.1 = (f32[21,16,128]{2,1,0:T(8,128)S(1)}, f32[21,16,128]{2,1,0:T(8,128)S(1)}, u32[]{:S(2)}, u32[]{:S(2)}) collective-permute-start(f32[21,16,128]{2,1,0:T(8,128)S(1)} %get-tuple-element.30), channel_id=1, source_target_pairs={{8,16},{16,8},{9,17},{17,9},{10,18},{18,10},{11,19},{19,11},{12,20... | collective-permute-start | bytes 516104 | tf_op jit(solution)/shard_map/ppermute | solution.py:702
  4.9 22.2 %collective-permute-start.2 = (f32[48,8,128]{2,1,0:T(8,128)S(1)}, f32[48,8,128]{2,1,0:T(8,128)S(1)}, u32[]{:S(2)}, u32[]{:S(2)}) collective-permute-start(f32[48,8,128]{2,1,0:T(8,128)S(1)} %get-tuple-element.31), channel_id=1, source_target_pairs={{0,1},{1,0},{2,3},{3,2},{4,5},{5,4},{6,7},{7,6},{8,9},{9,8},{10,11... | collective-permute-start | bytes 589832 | tf_op jit(solution)/shard_map/ppermute | solution.py:702
  5.0 22.2 %collective-permute-start.3 = (f32[48,8,128]{2,1,0:T(8,128)S(1)}, f32[48,8,128]{2,1,0:T(8,128)S(1)}, u32[]{:S(2)}, u32[]{:S(2)}) collective-permute-start(f32[48,8,128]{2,1,0:T(8,128)S(1)} %get-tuple-element.32), channel_id=1, source_target_pairs={{0,7},{1,2},{2,1},{3,4},{4,3},{5,6},{6,5},{7,0},{8,15},{9,10},{10,... | collective-permute-start | bytes 589832 | tf_op jit(solution)/shard_map/ppermute | solution.py:702
  8.6 18.5 %collective-permute-start.4 = (f32[44,8,128]{2,1,0:T(8,128)S(1)}, f32[44,8,128]{2,1,0:T(8,128)S(1)}, u32[]{:S(2)}, u32[]{:S(2)}) collective-permute-start(f32[44,8,128]{2,1,0:T(8,128)S(1)} %get-tuple-element.33), channel_id=1, source_target_pairs={{0,1},{1,0},{2,3},{3,2},{4,5},{5,4},{6,7},{7,6},{8,9},{9,8},{10,11... | collective-permute-start | bytes 540680 | tf_op jit(solution)/shard_map/ppermute | solution.py:702
  8.7 18.4 %collective-permute-start.5 = (f32[44,8,128]{2,1,0:T(8,128)S(1)}, f32[44,8,128]{2,1,0:T(8,128)S(1)}, u32[]{:S(2)}, u32[]{:S(2)}) collective-permute-start(f32[44,8,128]{2,1,0:T(8,128)S(1)} %get-tuple-element.34), channel_id=1, source_target_pairs={{0,7},{1,2},{2,1},{3,4},{4,3},{5,6},{6,5},{7,0},{8,15},{9,10},{10,... | collective-permute-start | bytes 540680 | tf_op jit(solution)/shard_map/ppermute | solution.py:702

commit v5 on v4

--- a/solution.py
+++ b/solution.py
@@ -434,12 +434,6 @@
 
     half = nx // 2 + HALO
     wide1 = 16
-    zero1 = jnp.zeros((ROWS1, nz), F32)
-    for i in range(half):
-        for ref in (rho1, b1, u1, v1, cy1):
-            ref[i] = zero1
-    for i in range(half):
-        tmp0[i] = zero0
 
     def rho_rows(i):
         return rho0[i, pl.ds(R0, wide), :]
@@ -651,8 +645,6 @@
     f1 = (cx1, cy1, cp1)
     first1, nx1 = HALO // 2, nx // 2
     wide1 = 16
-    for i in range(e1.shape[0]):
-        e1[i] = jnp.zeros((ROWS1, nz), F32)
     zero_row = jnp.zeros((1, nz), F32)
     for i in range(u1.shape[0]):
         for ref in (u1, x1):

time: 45.2 us -> 45.1 us (level)
  no operation moved by 1% of the time
where the time goes in v5:
time: 45.1 us; the launch traced here: 44.9 us
  blocking collectives  23.5 us (52%)
  Pallas kernels  11.1 us (25%)
  starting transfers between devices  9.18 us (20%)
  waiting for transfers between devices  1.09 us (2%)
    all_to_all x2, blocking collectives, gather(): return lax.all_to_all(value, AXES, 0, 0, tiled=True)  23.5 us
    ppermute x6, starting transfers between devices, swap(): return lax.ppermute(value, axis, exchange(count, parity, open_ends))  9.18 us
    pallas_call x1, Pallas kernels, body(): pl.pallas_call(pre_kernel, out_shape=(sds(devices, 8, nz), *[frame0] * 6,...  4.01 us
    pallas_call x1, Pallas kernels, body(): pl.pallas_call(post_kernel, out_shape=sds(nx, ny, nz), scratch_shapes=scr...  3.6 us
    pallas_call x1, Pallas kernels, body(): pl.pallas_call(functools.partial(source_kernel, (nx, ny, nz)), out_shape=...  2.34 us
    ppermute x6, waiting for transfers between devices, swap(): return lax.ppermute(value, axis, exchange(count, parity, open_ends))  1.09 us
    pallas_call x1, Pallas kernels, body(): pl.pallas_call(functools.partial(pack_kernel, devices), out_shape=(block,...  1.09 us
  transfers between devices with their start and end apart: 6, of which 1 were waited for; matrix products, arithmetic and copies ran while one was open for 0% of the time, Pallas kernels for 5%

profile of v5, /device:TPU:0, one launch (start us, length us, event | category | flops | bytes accessed | tf_op | source)
XLA Modules:
  0.0 44.9 jit_solution(6988954283507486551)
XLA Ops:
  0.0 1.1 %pack.1 = (f32[16,16,128]{2,1,0:T(8,128)S(1)}, f32[16,16,128]{2,1,0:T(8,128)S(1)}, f32[21,16,128]{2,1,0:T(8,128)S(1)}, f32[21,16,128]{2,1,0:T(8,128)S(1)}, f32[4...) custom-call(f32[16,16,128]{2,1,0:T(8,128)} %refs_0_.1, s32[16,16,128]{2,1,0:T(8,128)} %refs_1_.1, ...), custom_call_target="tpu_custom_call" | custom-call | tf_op jit(solution)/shard_map/pack/pallas_call | solution.py:715
  1.1 3.1 %collective-permute-start = (f32[21,16,128]{2,1,0:T(8,128)S(1)}, f32[21,16,128]{2,1,0:T(8,128)S(1)}, u32[]{:S(2)}, u32[]{:S(2)}) collective-permute-start(f32[21,16,128]{2,1,0:T(8,128)S(1)} %get-tuple-element.29), channel_id=1, source_target_pairs={{0,8},{8,0},{16,24},{24,16},{1,9},{9,1},{17,25},{25,17},{2,10},{10... | collective-permute-start | bytes 516104 | tf_op jit(solution)/shard_map/ppermute | solution.py:694
  4.2 0.7 %collective-permute-start.1 = (f32[21,16,128]{2,1,0:T(8,128)S(1)}, f32[21,16,128]{2,1,0:T(8,128)S(1)}, u32[]{:S(2)}, u32[]{:S(2)}) collective-permute-start(f32[21,16,128]{2,1,0:T(8,128)S(1)} %get-tuple-element.30), channel_id=1, source_target_pairs={{8,16},{16,8},{9,17},{17,9},{10,18},{18,10},{11,19},{19,11},{12,20... | collective-permute-start | bytes 516104 | tf_op jit(solution)/shard_map/ppermute | solution.py:694
  4.9 0.1 collective-permute-start.2
  5.0 2.5 %collective-permute-start.3 = (f32[48,8,128]{2,1,0:T(8,128)S(1)}, f32[48,8,128]{2,1,0:T(8,128)S(1)}, u32[]{:S(2)}, u32[]{:S(2)}) collective-permute-start(f32[48,8,128]{2,1,0:T(8,128)S(1)} %get-tuple-element.32), channel_id=1, source_target_pairs={{0,7},{1,2},{2,1},{3,4},{4,3},{5,6},{6,5},{7,0},{8,15},{9,10},{10,... | collective-permute-start | bytes 589832 | tf_op jit(solution)/shard_map/ppermute | solution.py:694
  7.5 1.1 %collective-permute-done.xa = f32[21,16,128]{2,1,0:T(8,128)S(1)} collective-permute-done((f32[21,16,128]{2,1,0:T(8,128)S(1)}, f32[21,16,128]{2,1,0:T(8,128)S(1)}, u32[]{:S(2)}, u32[]{:S(2)}) %collective-permute-start) | collective-permute-done | bytes 172064 | tf_op jit(solution)/shard_map/ppermute | solution.py:694
  8.6 0.0 collective-permute-done.1.xb
  8.6 0.1 collective-permute-start.4
  8.7 2.7 %collective-permute-start.5 = (f32[44,8,128]{2,1,0:T(8,128)S(1)}, f32[44,8,128]{2,1,0:T(8,128)S(1)}, u32[]{:S(2)}, u32[]{:S(2)}) collective-permute-start(f32[44,8,128]{2,1,0:T(8,128)S(1)} %get-tuple-element.34), channel_id=1, source_target_pairs={{0,7},{1,2},{2,1},{3,4},{4,3},{5,6},{6,5},{7,0},{8,15},{9,10},{10,... | collective-permute-start | bytes 540680 | tf_op jit(solution)/shard_map/ppermute | solution.py:694
  11.4 13.3 %all_to_all.16 = f32[32,4,128]{2,1,0:T(4,128)S(1)} all-to-all(f32[32,4,128]{2,1,0:T(4,128)S(1)} %bitcast.6), channel_id=1, replica_groups=mesh['stream'=4,'trans'=8] {'stream','trans'}, dimensions={0} | all-to-all | bytes 131072 | tf_op jit(solution)/shard_map/all_to_all | solution.py:698
  24.8 2.3 %source.1 = f32[36,48,128]{2,1,0:T(8,128)S(1)} custom-call(f32[128,128]{1,0:T(8,128)S(1)} %bitcast.5), custom_call_target="tpu_custom_call" | custom-call | tf_op jit(solution)/shard_map/source/pallas_call | solution.py:751
  27.1 0.0 collective-permute-done.2.ya
  27.1 0.0 collective-permute-done.3.yb
  27.1 0.0 collective-permute-done.4.ca
  27.1 0.0 collective-permute-done.5.cb
  27.2 4.0 %presmooth.1 = (f32[32,8,128]{2,1,0:T(8,128)S(1)}, f32[40,48,128]{2,1,0:T(8,128)S(1)}, f32[40,48,128]{2,1,0:T(8,128)S(1)}, f32[40,48,128]{2,1,0:T(8,128)S(1)}, f...) custom-call(f32[16,16,128]{2,1,0:T(8,128)S(1)} %get-tuple-element.27, ...), custom_call_target="tpu_custom_call" | custom-call | tf_op jit(solution)/shard_map/presmooth/pallas_call | solution.py:764
  31.2 10.2 %all_to_all.17.slots = f32[32,8,128]{2,1,0:T(8,128)S(1)} all-to-all(f32[32,8,128]{2,1,0:T(8,128)S(1)} %get-tuple-element.36), channel_id=1, replica_groups=mesh['stream'=4,'trans'=8] {'stream','trans'}, dimensions={0} | all-to-all | bytes 262144 | tf_op jit(solution)/shard_map/all_to_all | solution.py:698
  41.3 3.6 %postsmooth.1 = f32[16,16,128]{2,1,0:T(8,128)} custom-call(f32[32,8,128]{2,1,0:T(8,128)S(1)} %all_to_all.17.slots, f32[40,48,128]{2,1,0:T(8,128)S(1)} %get-tuple-element.37.v0, f32[40,48,128]{2,1,0:T(8,128)S(1)} %get-tuple-element.38.b0, f32[40,48,128]{2,1,0:T(8,128)S(1)} %get-tuple-element.39.w0, f32[40,48,128]{2,1,0:T(8,128)S(1)} %get-tuple-element.40.cx0, ...), custom_call_target="tpu_custom_call" | custom-call | tf_op jit(solution)/shard_map/postsmooth/pallas_call | solution.py:786
  (1 shorter events, 0.0 us)
Async XLA Ops:
  1.1 7.5 %collective-permute-start = (f32[21,16,128]{2,1,0:T(8,128)S(1)}, f32[21,16,128]{2,1,0:T(8,128)S(1)}, u32[]{:S(2)}, u32[]{:S(2)}) collective-permute-start(f32[21,16,128]{2,1,0:T(8,128)S(1)} %get-tuple-element.29), channel_id=1, source_target_pairs={{0,8},{8,0},{16,24},{24,16},{1,9},{9,1},{17,25},{25,17},{2,10},{10... | collective-permute-start | bytes 516104 | tf_op jit(solution)/shard_map/ppermute | solution.py:694
  4.2 4.4 %collective-permute-start.1 = (f32[21,16,128]{2,1,0:T(8,128)S(1)}, f32[21,16,128]{2,1,0:T(8,128)S(1)}, u32[]{:S(2)}, u32[]{:S(2)}) collective-permute-start(f32[21,16,128]{2,1,0:T(8,128)S(1)} %get-tuple-element.30), channel_id=1, source_target_pairs={{8,16},{16,8},{9,17},{17,9},{10,18},{18,10},{11,19},{19,11},{12,20... | collective-permute-start | bytes 516104 | tf_op jit(solution)/shard_map/ppermute | solution.py:694
  4.9 22.2 %collective-permute-start.2 = (f32[48,8,128]{2,1,0:T(8,128)S(1)}, f32[48,8,128]{2,1,0:T(8,128)S(1)}, u32[]{:S(2)}, u32[]{:S(2)}) collective-permute-start(f32[48,8,128]{2,1,0:T(8,128)S(1)} %get-tuple-element.31), channel_id=1, source_target_pairs={{0,1},{1,0},{2,3},{3,2},{4,5},{5,4},{6,7},{7,6},{8,9},{9,8},{10,11... | collective-permute-start | bytes 589832 | tf_op jit(solution)/shard_map/ppermute | solution.py:694
  5.0 22.2 %collective-permute-start.3 = (f32[48,8,128]{2,1,0:T(8,128)S(1)}, f32[48,8,128]{2,1,0:T(8,128)S(1)}, u32[]{:S(2)}, u32[]{:S(2)}) collective-permute-start(f32[48,8,128]{2,1,0:T(8,128)S(1)} %get-tuple-element.32), channel_id=1, source_target_pairs={{0,7},{1,2},{2,1},{3,4},{4,3},{5,6},{6,5},{7,0},{8,15},{9,10},{10,... | collective-permute-start | bytes 589832 | tf_op jit(solution)/shard_map/ppermute | solution.py:694
  8.6 18.5 %collective-permute-start.4 = (f32[44,8,128]{2,1,0:T(8,128)S(1)}, f32[44,8,128]{2,1,0:T(8,128)S(1)}, u32[]{:S(2)}, u32[]{:S(2)}) collective-permute-start(f32[44,8,128]{2,1,0:T(8,128)S(1)} %get-tuple-element.33), channel_id=1, source_target_pairs={{0,1},{1,0},{2,3},{3,2},{4,5},{5,4},{6,7},{7,6},{8,9},{9,8},{10,11... | collective-permute-start | bytes 540680 | tf_op jit(solution)/shard_map/ppermute | solution.py:694
  8.7 18.4 %collective-permute-start.5 = (f32[44,8,128]{2,1,0:T(8,128)S(1)}, f32[44,8,128]{2,1,0:T(8,128)S(1)}, u32[]{:S(2)}, u32[]{:S(2)}) collective-permute-start(f32[44,8,128]{2,1,0:T(8,128)S(1)} %get-tuple-element.34), channel_id=1, source_target_pairs={{0,7},{1,2},{2,1},{3,4},{4,3},{5,6},{6,5},{7,0},{8,15},{9,10},{10,... | collective-permute-start | bytes 540680 | tf_op jit(solution)/shard_map/ppermute | solution.py:694
